TPU v7x, 512 devices: a whole 4x8x8 slice. The times are simulated.
512 devices in a mesh: seq: 64 (over x, y, z_lo), tp: 8 (over z_hi, core).
Axes of the slice: x: 4, y: 8, z: 8 (z_hi: 4, z_lo: 2; z = z_hi * 2 + z_lo), core: 2. Of those that a mesh axis runs over, the one named last changes fastest.
Arguments:
- queries: bfloat16 [16384, 3072], P(('seq', 'tp')), may hold values from -42 to 42
- keys: bfloat16 [16384, 3072], P(('seq', 'tp')), may hold values from -6 to 6
- values: bfloat16 [16384, 3072], P(('seq', 'tp')), may hold values from -6 to 6
- pool_keys: bfloat16 [64, 128, 3072], P('seq', None, 'tp'), may hold values from -6 to 6
- pool_values: bfloat16 [64, 128, 3072], P('seq', None, 'tp'), may hold values from -6 to 6
- page_table: int32 [64], replicated, may hold values from 0 to 63, each once
- lengths: int32 [128], replicated, may hold values from 1 to 256, 16384 in all
- group_of: int32 [128], replicated, may hold values from 0 to 1
Outputs:
- context: bfloat16 [16384, 3072], P(('seq', 'tp'))
- new_keys: bfloat16 [16384, 3072], P('seq', 'tp')
- new_values: bfloat16 [16384, 3072], P('seq', 'tp')
Inputs may be any that keep to these rules, and one draw needn't show every extreme that they name: `page_table`: each of the 64 slots appears once; entries g * 32 to (g + 1) * 32 - 1 are group g's pages; slot s lies on index s of seq. The lengths sum to 16384; each request's suffix tokens follow those of the requests before it.
All inputs are finite; a program needn't handle non-finite values.
Results may differ from a plain program's by a relative error of at most 0.0055.
Values may be sent and summed in bfloat16 or wider, within the bound.
A program may use at most 64 MiB of HBM per device.

v0:
```python
import math

import jax
import jax.numpy as jnp
from jax import lax
from jax.sharding import PartitionSpec as P

HD = 96
ROT = 24


def shifted(block, axis, distance):
    devices = range(lax.axis_size(axis))
    route = [(i - distance, i) for i in devices if i - distance in devices]
    return lax.ppermute(block, axis, route)


def rotate(matrix, position):
    count = matrix.shape[0]
    split_heads = matrix.reshape(count, -1, HD)
    half_rot = ROT // 2
    inverse_freq = 10000.0 ** (-(jnp.arange(half_rot, dtype=jnp.float32) * 2.0 / ROT))
    angles = position.astype(jnp.float32)[:, None] * inverse_freq[None, :]
    cosine = jnp.cos(angles)[:, None, :]
    sine = jnp.sin(angles)[:, None, :]
    first_half = split_heads[..., :half_rot]
    second_half = split_heads[..., half_rot:ROT]
    rest_dims = split_heads[..., ROT:]
    turned = jnp.concatenate(
        [
            first_half * cosine - second_half * sine,
            second_half * cosine + first_half * sine,
            rest_dims,
        ],
        axis=-1,
    )
    return turned.reshape(count, -1)


def local(queries, keys, values, pool_keys, pool_values, page_table, lengths, group_of):
    seq_count = lax.axis_size("seq")
    head_queries, head_keys, head_values = (
        lax.all_to_all(queries, "tp", split_axis=1, concat_axis=0, tiled=True),
        lax.all_to_all(keys, "tp", split_axis=1, concat_axis=0, tiled=True),
        lax.all_to_all(values, "tp", split_axis=1, concat_axis=0, tiled=True),
    )
    tok_rows = head_queries.shape[0]
    channels = head_queries.shape[1]
    heads_here = channels // HD
    page_rows = pool_keys.shape[1]
    slots_here = pool_keys.shape[0]
    slot_count = slots_here * seq_count
    pages_group = slot_count // 2
    prefix_len = pages_group * page_rows
    request_count = lengths.shape[0]
    request_ends = jnp.cumsum(lengths)
    request_starts = request_ends - lengths
    request_ids = jnp.arange(request_count, dtype=jnp.int32)
    my_index = lax.axis_index("seq")
    row_base = my_index * tok_rows
    query_rows = row_base + jnp.arange(tok_rows, dtype=jnp.int32)
    request = jnp.sum((query_rows[:, None] >= request_ends[None, :]).astype(jnp.int32), axis=1)
    one_hot = (request[:, None] == request_ids[None, :]).astype(jnp.int32)
    offset = query_rows - jnp.sum(one_hot * request_starts[None, :], axis=1)
    group = jnp.sum(one_hot * group_of[None, :], axis=1)
    position = prefix_len + offset
    rot_queries = rotate(head_queries.astype(jnp.float32), position).astype(jnp.bfloat16)
    rot_keys = rotate(head_keys.astype(jnp.float32), position).astype(jnp.bfloat16)
    earlier_keys, earlier_values = shifted((rot_keys, head_values), "seq", 1)
    earlier_rows = query_rows - tok_rows
    earlier_request = jnp.sum(
        (earlier_rows[:, None] >= request_ends[None, :]).astype(jnp.int32), axis=1
    )
    suffix_keys = jnp.concatenate([earlier_keys, rot_keys], axis=0)
    suffix_values = jnp.concatenate([earlier_values, head_values], axis=0)
    key_rows = jnp.concatenate([earlier_rows, query_rows], axis=0)
    key_request = jnp.concatenate([earlier_request, request], axis=0)
    suffix_mask = (
        (key_request[None, :] == request[:, None])
        & (key_rows[None, :] <= query_rows[:, None])
        & (key_rows[None, :] >= 0)
    )
    slot_ids = jnp.arange(slot_count, dtype=jnp.int32)
    member = (page_table[None, :] == slot_ids[:, None]) & (slot_ids[None, :] >= pages_group)
    slot_group = jnp.any(member, axis=1).astype(jnp.int32)
    score_scale = HD ** (-0.5)

    def attend(state, query_block, key_block, value_block, allowed):
        row_max, total, accum = state
        query_heads = query_block.reshape(query_block.shape[0], heads_here, HD)
        key_heads = key_block.reshape(key_block.shape[0], heads_here, HD)
        value_heads = value_block.reshape(value_block.shape[0], heads_here, HD)
        scores = (
            jnp.einsum("qhd,khd->hqk", query_heads, key_heads, preferred_element_type=jnp.float32)
            * score_scale
        )
        scores = jnp.where(allowed[None], scores, -1e30)
        new_max = jnp.maximum(row_max, jnp.max(scores, axis=-1))
        weights = jnp.where(allowed[None], jnp.exp(scores - new_max[..., None]), 0.0)
        factor = jnp.exp(row_max - new_max)
        new_total = total * factor + jnp.sum(weights, axis=-1)
        weights_bf16 = weights.astype(jnp.bfloat16)
        new_accum = accum * factor[..., None] + jnp.einsum(
            "hqk,khd->hqd", weights_bf16, value_heads, preferred_element_type=jnp.float32
        )
        return (new_max, new_total, new_accum)

    initial = (
        jnp.full((heads_here, tok_rows), -1e30, jnp.float32),
        jnp.zeros((heads_here, tok_rows), jnp.float32),
        jnp.zeros((heads_here, tok_rows, HD), jnp.float32),
    )
    state = initial
    piece_keys = lax.all_gather(pool_keys, "seq", axis=0, tiled=True)
    piece_slots = piece_keys.shape[0]
    piece_ids = jnp.arange(piece_slots, dtype=jnp.int32)
    piece_group = jnp.sum(
        (piece_ids[:, None] == slot_ids[None, :]).astype(jnp.int32) * slot_group[None, :], axis=1
    )
    block_pages = math.gcd(piece_slots, 4)
    block_count = piece_slots // block_pages
    keys_blocked = piece_keys.reshape(block_count, block_pages * page_rows, channels)
    values_blocked = lax.all_gather(pool_values, "seq", axis=0, tiled=True).reshape(
        block_count, block_pages * page_rows, channels
    )
    groups_blocked = piece_group.reshape(block_count, block_pages)

    def one_step(running, item):
        key_block, value_block, group_block = item
        key_group = jnp.repeat(group_block, page_rows)
        allowed = group[:, None] == key_group[None, :]
        return (attend(running, rot_queries, key_block, value_block, allowed), None)

    state, _ = lax.scan(one_step, state, (keys_blocked, values_blocked, groups_blocked))
    state = attend(state, rot_queries, suffix_keys, suffix_values, suffix_mask)
    final_max, final_total, final_accum = state
    context_heads = (
        (final_accum / final_total[..., None])
        .transpose(1, 0, 2)
        .reshape(tok_rows, channels)
        .astype(jnp.bfloat16)
    )
    context = lax.all_to_all(context_heads, "tp", split_axis=0, concat_axis=1, tiled=True)
    return (context, rot_keys, head_values)


def solution(mesh):
    return jax.shard_map(
        local,
        mesh=mesh,
        in_specs=(
            P(("seq", "tp"), None),
            P(("seq", "tp"), None),
            P(("seq", "tp"), None),
            P("seq", None, "tp"),
            P("seq", None, "tp"),
            P(),
            P(),
            P(),
        ),
        out_specs=(P(("seq", "tp"), None), P("seq", "tp"), P("seq", "tp")),
        check_vma=False,
    )
```

profile of v0, /device:TPU:1, one launch (start us, length us, event | category | flops | bytes accessed | tf_op | source)
XLA Modules:
  0.0 726.4 jit_solution(3364903707367896653)
XLA Ops:
  7.2 0.7 all-gather.3.cloned.1.call-update
  8.0 0.7 all-gather.5.cloned.1.call-update
  8.7 1.6 copy.109
  10.3 11.8 %all-to-all-start = ((bf16[32,8,384]{2,0,1:T(8,128)(2,1)}), bf16[32,8,384]{2,0,1:T(8,128)(2,1)S(1)}, u32[]{:S(2)}, u32[]{:S(2)}) async-start(bf16[32,8,384]{2,0,1:T(8,128)(2,1)} %bitcast.52), calls=%async_computation | async-start | bytes 393216 | tf_op jit(solution)/shard_map/all_to_all | solution.py:43
  22.1 0.8 copy.76
  23.1 0.7 sub.42
  24.1 0.9 select_reduce_fusion.1
  25.0 1.6 copy.108
  26.6 0.8 fusion.28
  27.5 4.6 all-to-all-done
  32.1 4.6 all-to-all-start.1
  36.8 0.7 copy.107
  37.7 12.3 %all-to-all-done.1 = bf16[32,8,384]{2,0,1:T(8,128)(2,1)S(1)} async-done(((bf16[32,8,384]{2,0,1:T(8,128)(2,1)}), bf16[32,8,384]{2,0,1:T(8,128)(2,1)S(1)}, u32[]{:S(2)}, u32[]{:S(2)}) %all-to-all-start.1) | async-done | bytes 196640 | tf_op jit(solution)/shard_map/all_to_all | solution.py:44
  50.0 3.7 all-to-all-start.2
  54.8 9.4 %all-to-all-done.2 = bf16[32,8,384]{2,0,1:T(8,128)(2,1)S(1)} async-done(((bf16[32,8,384]{2,0,1:T(8,128)(2,1)}), bf16[32,8,384]{2,0,1:T(8,128)(2,1)S(1)}, u32[]{:S(2)}, u32[]{:S(2)}) %all-to-all-start.2) | async-done | bytes 196640 | tf_op jit(solution)/shard_map/all_to_all | solution.py:45
  64.3 3.8 collective-permute-start.1
  68.5 0.6 pad_maximum_fusion.1
  69.3 3.3 collective-permute-start
  74.4 5.3 collective-permute-done
  79.7 1.9 fusion.13
  81.7 207.7 %all-gather.3.cloned.1.call-done = bf16[64,128,384]{2,1,0:T(8,128)(2,1)} async-done(((bf16[1,128,384]{2,1,0:T(8,128)(2,1)}), bf16[64,128,384]{2,1,0:T(8,128)(2,1)}) %all-gather.3.cloned.1.call-update) | async-done | bytes 6291472 | tf_op jit(solution)/shard_map/all_gather | solution.py:114
  289.4 305.0 %all-gather.5.cloned.1.call-done = bf16[64,128,384]{2,1,0:T(8,128)(2,1)} async-done(((bf16[1,128,384]{2,1,0:T(8,128)(2,1)}), bf16[64,128,384]{2,1,0:T(8,128)(2,1)}) %all-gather.5.cloned.1.call-update) | async-done | bytes 6291472 | tf_op jit(solution)/shard_map/all_gather | solution.py:123
  594.4 59.1 %while.15 = (s32[]{:T(128)}, f32[4,256]{1,0:T(4,128)S(1)}, f32[4,256]{1,0:T(4,128)S(1)}, f32[4,256,96]{1,2,0:T(8,128)S(1)}, s32[256]{0:T(256)S(1)}, /*index=5*/s...) while((s32[]{:T(128)}, f32[4,256]{1,0:T(4,128)S(1)}, ...), condition=%wide.region_9.10_spmd.clone, body=%wide.region_6.0_spmd.clone.sunk | while | flops 208573440 | bytes 11801785 | solution.py:134
  594.6 1.2 constant_dynamic-slice_fusion.4
  597.3 0.7 convolution_add_fusion.3
  598.3 1.2 constant_dynamic-slice_fusion.4
  601.0 0.7 convolution_add_fusion.3
  602.0 1.2 constant_dynamic-slice_fusion.4
  603.6 0.6 fusion.53
  604.7 0.7 convolution_add_fusion.3
  605.7 1.2 constant_dynamic-slice_fusion.4
  608.4 0.7 convolution_add_fusion.3
  609.4 1.2 constant_dynamic-slice_fusion.4
  612.1 0.7 convolution_add_fusion.3
  613.1 1.2 constant_dynamic-slice_fusion.4
  615.8 0.7 convolution_add_fusion.3
  616.8 1.2 constant_dynamic-slice_fusion.4
  619.5 0.7 convolution_add_fusion.3
  620.5 1.2 constant_dynamic-slice_fusion.4
  623.2 0.7 convolution_add_fusion.3
  624.2 1.2 constant_dynamic-slice_fusion.4
  626.9 0.7 convolution_add_fusion.3
  627.9 1.2 constant_dynamic-slice_fusion.4
  630.6 0.7 convolution_add_fusion.3
  631.6 1.2 constant_dynamic-slice_fusion.4
  634.3 0.7 convolution_add_fusion.3
  635.3 1.2 constant_dynamic-slice_fusion.4
  638.0 0.7 convolution_add_fusion.3
  639.0 1.2 constant_dynamic-slice_fusion.4
  641.7 0.7 convolution_add_fusion.3
  642.7 1.2 constant_dynamic-slice_fusion.4
  645.4 0.7 convolution_add_fusion.3
  646.4 1.2 constant_dynamic-slice_fusion.4
  649.1 0.7 convolution_add_fusion.3
  650.1 1.2 constant_dynamic-slice_fusion.4
  652.8 0.7 convolution_add_fusion.3
  653.6 2.5 fusion.14
  656.1 0.8 fusion.18
  657.1 0.9 convert_element_type.86
  658.0 50.2 %all-to-all-start.3 = ((bf16[8,32,384]{2,1,0:T(8,128)(2,1)}), bf16[8,32,384]{2,1,0:T(8,128)(2,1)S(1)}, u32[]{:S(2)}, u32[]{:S(2)}) async-start(bf16[8,32,384]{2,1,0:T(8,128)(2,1)} %convert_element_type.86), calls=%async_computation.3 | async-start | bytes 393216 | tf_op jit(solution)/shard_map/all_to_all | solution.py:143
  708.1 0.8 copy.93
  708.9 9.2 %all-to-all-done.3 = bf16[8,32,384]{2,1,0:T(8,128)(2,1)S(1)} async-done(((bf16[8,32,384]{2,1,0:T(8,128)(2,1)}), bf16[8,32,384]{2,1,0:T(8,128)(2,1)S(1)}, u32[]{:S(2)}, u32[]{:S(2)}) %all-to-all-start.3) | async-done | bytes 196640 | tf_op jit(solution)/shard_map/all_to_all | solution.py:143
  718.2 0.7 copy.103
  718.9 0.7 copy.127
  (208 shorter events, 31.5 us)
Async XLA Ops:
  7.2 29.6 %copy-start.1 = (bf16[32,3072]{1,0:T(8,128)(2,1)S(1)}, bf16[32,3072]{1,0:T(8,128)(2,1)}, u32[]{:S(2)}) copy-start(bf16[32,3072]{1,0:T(8,128)(2,1)} %param.12) | copy-start | bytes 589828
  7.2 282.2 %all-gather.3.cloned.1.call-start = ((), (), s32[]{:S(2)}) async-start(), calls=%async_computation.4 | async-start | bytes 6389760 | tf_op jit(solution)/shard_map/all_gather | solution.py:114
  7.9 586.5 %all-gather.5.cloned.1.call-start = ((), (), s32[]{:S(2)}) async-start(), calls=%async_computation.5 | async-start | bytes 6389760 | tf_op jit(solution)/shard_map/all_gather | solution.py:123
  10.3 21.8 %all-to-all-start = ((bf16[32,8,384]{2,0,1:T(8,128)(2,1)}), bf16[32,8,384]{2,0,1:T(8,128)(2,1)S(1)}, u32[]{:S(2)}, u32[]{:S(2)}) async-start(bf16[32,8,384]{2,0,1:T(8,128)(2,1)} %bitcast.52), calls=%async_computation | async-start | bytes 393216 | tf_op jit(solution)/shard_map/all_to_all | solution.py:43
  32.1 17.9 %all-to-all-start.1 = ((bf16[32,8,384]{2,0,1:T(8,128)(2,1)}), bf16[32,8,384]{2,0,1:T(8,128)(2,1)S(1)}, u32[]{:S(2)}, u32[]{:S(2)}) async-start(bf16[32,8,384]{2,0,1:T(8,128)(2,1)} %bitcast.51), calls=%async_computation.1 | async-start | bytes 393216 | tf_op jit(solution)/shard_map/all_to_all | solution.py:44
  50.0 14.3 %all-to-all-start.2 = ((bf16[32,8,384]{2,0,1:T(8,128)(2,1)}), bf16[32,8,384]{2,0,1:T(8,128)(2,1)S(1)}, u32[]{:S(2)}, u32[]{:S(2)}) async-start(bf16[32,8,384]{2,0,1:T(8,128)(2,1)} %bitcast.50), calls=%async_computation.2 | async-start | bytes 393216 | tf_op jit(solution)/shard_map/all_to_all | solution.py:45
  64.3 9.9 %collective-permute-start.1 = (bf16[256,384]{1,0:T(8,128)(2,1)S(1)}, bf16[256,384]{1,0:T(8,128)(2,1)S(1)}, u32[]{:S(2)}, u32[]{:S(2)}) collective-permute-start(bf16[256,384]{1,0:T(8,128)(2,1)S(1)} %bitcast.79), channel_id=1, source_target_pairs={{0,8},{8,16},{16,24},{24,32},{32,40},{40,48},{48,56},{56,64},{64,7... | collective-permute-start | bytes 589832 | tf_op jit(solution)/shard_map/ppermute | solution.py:15
  69.3 10.4 %collective-permute-start = (bf16[256,384]{0,1:T(8,128)(2,1)S(1)}, bf16[256,384]{0,1:T(8,128)(2,1)S(1)}, u32[]{:S(2)}, u32[]{:S(2)}) collective-permute-start(bf16[256,384]{0,1:T(8,128)(2,1)S(1)} %bitcast.82), channel_id=1, source_target_pairs={{0,8},{8,16},{16,24},{24,32},{32,40},{40,48},{48,56},{56,64},{64,7... | collective-permute-start | bytes 589832 | tf_op jit(solution)/shard_map/ppermute | solution.py:15
  653.5 2.6 copy-start
  658.0 60.2 %all-to-all-start.3 = ((bf16[8,32,384]{2,1,0:T(8,128)(2,1)}), bf16[8,32,384]{2,1,0:T(8,128)(2,1)S(1)}, u32[]{:S(2)}, u32[]{:S(2)}) async-start(bf16[8,32,384]{2,1,0:T(8,128)(2,1)} %convert_element_type.86), calls=%async_computation.3 | async-start | bytes 393216 | tf_op jit(solution)/shard_map/all_to_all | solution.py:143
Sparse Core Ops, SparseCore 0:
  10.1 279.2 all-gather.2
  291.5 302.8 all-gather.4
where the time goes:
time: 727 us; the launch traced here: 726 us
  waiting for transfers between devices  555 us (76%)
  starting transfers between devices  77.5 us (11%)
  local copies, waits for them, and re-layouts  37.7 us (5%)
  matrix products  22.9 us (3%)
  other arithmetic  17.8 us (2%)
  between operations  14.3 us (2%)
    all_gather x1, waiting for transfers between devices, local(): lax.all_gather(pool_values, 'seq', axis=0, tiled=True)  305 us
    all_gather x1, waiting for transfers between devices, local(): piece_keys = lax.all_gather(pool_keys, 'seq', axis=0, tiled=True)  208 us
    all_to_all x1, starting transfers between devices, local(): lax.all_to_all(context_heads, 'tp', split_axis=0, concat_axis=1, tiled=True)  50.2 us
    dynamic_slice x48, local copies, waits for them, and re-layouts, local(): lax.scan(one_step, state, (keys_blocked, values_blocked, groups_blocked))  25.3 us
  transfers between devices with their start and end apart: 8, of which 7 were waited for; matrix products, arithmetic and copies ran while one was open for 2% of the time, Pallas kernels for 0%

commit v1 on v0

v1 whole, which is shorter than its diff:
```python
import jax
import jax.numpy as jnp
from jax import lax
from jax.experimental import pallas as pl
from jax.experimental.pallas import tpu as pltpu
from jax.sharding import PartitionSpec as P

MESH = pl.DeviceIdType.MESH
HD = 96
ROT = 24
HALF = ROT // 2
HEADS = 4
CH = HEADS * HD
TOK = 256
PART = 32
NT = 8
NX, NY, NZ = 4, 8, 2
COL = NY * NZ
PAGE = 128
KEYS = COL * PAGE
SEQ = NX * NY * NZ
NEG = -1e30
EXP_SCALE = HD**-0.5 * 1.4426950408889634
VMEM = pltpu.VMEM


def where_am_i():
    s = lax.axis_index("seq")
    t = lax.axis_index("tp")
    x = s // COL
    y = (s // NZ) % NY
    z = s % NZ
    return s, t, x, y, z


def greet(peers):
    barrier = pltpu.get_barrier_semaphore()
    for peer in peers:
        pl.semaphore_signal(barrier, inc=1, device_id=peer, device_id_type=MESH)
    pl.semaphore_wait(barrier, len(peers))


def remote(src, dst, send, recv, peer):
    return pltpu.make_async_remote_copy(
        src_ref=src, dst_ref=dst, send_sem=send, recv_sem=recv, device_id=peer, device_id_type=MESH
    )


def spread_kernel(
    q_ref, k_ref, v_ref, pk_ref, pv_ref,
    qa_ref, k2_ref, v2_ref, gk_ref, gv_ref,
    a_send, a_recv, z_send, z_recv, r_send, r_recv, x_send, x_recv, s_send, s_recv, loc,
):
    s, t, x, y, z = where_am_i()
    col = s % COL
    partner = (s + 1 - 2 * z, t)
    up = (x * COL + ((y + 1) % NY) * NZ + z, t)
    down = (x * COL + ((y + NY - 1) % NY) * NZ + z, t)
    after = ((s + 1) % SEQ, t)
    before = ((s + SEQ - 1) % SEQ, t)
    tps = [(s, (t + j) % NT) for j in range(1, NT)]
    xs = [(((x + j) % NX) * COL + col, t) for j in range(1, NX)]
    greet([partner, up, down, after, before] + tps + xs)

    pending = []

    def go(copy):
        copy.start()
        pending.append(copy)
        return copy

    zk = go(remote(pk_ref.at[0], gk_ref.at[y, z], z_send.at[0], z_recv.at[0], partner))
    zv = go(remote(pv_ref.at[0], gv_ref.at[y, z], z_send.at[1], z_recv.at[1], partner))

    def rows(ref, kind):
        return ref.at[x if kind == 0 else 1, pl.ds(pl.multiple_of(t * PART, PART), PART), :]

    def lanes(ref, index):
        return ref.at[:, pl.ds(pl.multiple_of(index * CH, 128), CH)]

    kinds = [(q_ref, qa_ref), (k_ref, k2_ref), (v_ref, v2_ref)]
    swaps = []
    for kind, (src, dst) in enumerate(kinds):
        swaps.append(
            [
                go(remote(lanes(src, tps[j][1]), rows(dst, kind), a_send.at[kind, j], a_recv.at[kind, j], tps[j]))
                for j in range(NT - 1)
            ]
        )
    own = [
        pltpu.make_async_copy(pk_ref.at[0], gk_ref.at[y, z], loc.at[0]),
        pltpu.make_async_copy(pv_ref.at[0], gv_ref.at[y, z], loc.at[1]),
    ] + [
        pltpu.make_async_copy(lanes(src, t), rows(dst, kind), loc.at[2 + kind])
        for kind, (src, dst) in enumerate(kinds)
    ]
    for copy in own:
        copy.start()
    for copy in own:
        copy.wait()
    zk.wait_recv()
    zv.wait_recv()

    flows = [(gk_ref, 0, 4), (gv_ref, 0, 3), (gk_ref, 1, 3), (gv_ref, 1, 4)]
    last = [None] * len(flows)

    def hop(step):
        for index, (ref, way, hops) in enumerate(flows):
            if step > 0 and last[index] is not None:
                last[index].wait_recv()
                last[index] = None
            if step < hops:
                at = (y + NY - step) % NY if way == 0 else (y + step) % NY
                last[index] = go(
                    remote(
                        ref.at[at], ref.at[at], r_send.at[index, step], r_recv.at[index, step], up if way == 0 else down
                    )
                )

    hop(0)
    for copy in swaps[0]:
        copy.wait_recv()
    across = [
        go(remote(qa_ref.at[x], qa_ref.at[x], x_send.at[j], x_recv.at[j], xs[j])) for j in range(NX - 1)
    ]
    hop(1)
    for copy in swaps[1] + swaps[2]:
        copy.wait_recv()
    shifts = [
        go(remote(ref.at[1], ref.at[0], s_send.at[i], s_recv.at[i], after)) for i, ref in enumerate((k2_ref, v2_ref))
    ]
    hop(2)
    hop(3)
    hop(4)
    for copy in across + shifts:
        copy.wait_recv()
    for copy in pending:
        copy.wait_send()


def spread(q, k, v, pk, pv):
    bf = jnp.bfloat16
    dma = pltpu.SemaphoreType.DMA
    return pl.pallas_call(
        spread_kernel,
        out_shape=(
            jax.ShapeDtypeStruct((NX, TOK, CH), bf),
            jax.ShapeDtypeStruct((2, TOK, CH), bf),
            jax.ShapeDtypeStruct((2, TOK, CH), bf),
            jax.ShapeDtypeStruct((NY, NZ, PAGE, CH), bf),
            jax.ShapeDtypeStruct((NY, NZ, PAGE, CH), bf),
        ),
        in_specs=[pl.BlockSpec(memory_space=VMEM)] * 5,
        out_specs=[pl.BlockSpec(memory_space=VMEM)] * 5,
        scratch_shapes=[
            dma((3, NT - 1)), dma((3, NT - 1)),
            dma((2,)), dma((2,)),
            dma((4, 4)), dma((4, 4)),
            dma((NX - 1,)), dma((NX - 1,)),
            dma((2,)), dma((2,)),
            dma((5,)),
        ],
        compiler_params=pltpu.CompilerParams(collective_id=0, has_side_effects=True),
        name="spread",
    )(q, k, v, pk, pv)


def turn(matrix, cosine, sine):
    parts = []
    for h in range(HEADS):
        lead = matrix[h * HD : h * HD + ROT]
        other = jnp.concatenate([lead[HALF:], lead[:HALF]], axis=0)
        parts += [lead * cosine + other * sine, matrix[h * HD + ROT : (h + 1) * HD]]
    return jnp.concatenate(parts, axis=0)


def widen(columns, h):
    start = h * HD - (h // 2) * 128
    pieces = []
    if start:
        pieces.append(jnp.zeros((start, TOK), jnp.bfloat16))
    pieces.append(columns[h * HD : (h + 1) * HD])
    if start + HD < 256:
        pieces.append(jnp.zeros((256 - start - HD, TOK), jnp.bfloat16))
    return jnp.concatenate(pieces, axis=0)


def attend_kernel(
    qa_ref, k2_ref, v2_ref, gk_ref, gv_ref, cos_ref, sin_ref, bias_ref, offset_ref,
    o_ref, stat_ref, osuf_ref, ssuf_ref, newk_ref,
    vt_ref, vs_ref, ks_ref,
):
    me = lax.axis_index("seq") // COL
    for b in range(2):
        turned = turn(k2_ref[b].astype(jnp.float32).T, cos_ref[b], sin_ref[b])
        turned = turned.T.astype(jnp.bfloat16)
        ks_ref[b * TOK : (b + 1) * TOK, :] = turned
        vs_ref[:, b * TOK : (b + 1) * TOK] = v2_ref[b].astype(jnp.float32).T.astype(jnp.bfloat16)
    newk_ref[...] = ks_ref[TOK:, :]
    for b in range(KEYS // 256):
        vt_ref[:, b * 256 : (b + 1) * 256] = (
            gv_ref[b * 256 : (b + 1) * 256, :].astype(jnp.float32).T.astype(jnp.bfloat16)
        )

    def queries(b):
        return turn(qa_ref[b].astype(jnp.float32).T, cos_ref[2 + b], sin_ref[2 + b]).astype(jnp.bfloat16)

    def finish(scores, values):
        top = jnp.max(scores, axis=0, keepdims=True)
        weights = jnp.exp2((scores - top) * EXP_SCALE)
        total = jnp.sum(weights, axis=0, keepdims=True)
        summed = jnp.dot(values, weights.astype(jnp.bfloat16), preferred_element_type=jnp.float32)
        return top, total, summed / total

    def one_block(b, carry):
        columns = queries(b)
        bias = bias_ref[b]
        for h in range(HEADS):
            lane = (h // 2) * 128
            scores = jnp.dot(gk_ref[:, lane : lane + 256], widen(columns, h), preferred_element_type=jnp.float32)
            scores = (scores.reshape(COL, PAGE, TOK) + bias[:, None, :]).reshape(KEYS, TOK)
            top, total, out = finish(scores, vt_ref[h * HD : (h + 1) * HD, :])
            o_ref[b, h * HD : (h + 1) * HD, :] = out.astype(jnp.bfloat16)
            stat_ref[b, h : h + 1, :] = top
            stat_ref[b, HEADS + h : HEADS + h + 1, :] = total
        return carry

    lax.fori_loop(0, NX, one_block, 0)

    columns = queries(me)
    token = lax.broadcasted_iota(jnp.int32, (2 * TOK, TOK), 1) + TOK
    key = lax.broadcasted_iota(jnp.int32, (2 * TOK, TOK), 0)
    allowed = (key <= token) & (key >= token - offset_ref[...])
    for h in range(HEADS):
        lane = (h // 2) * 128
        scores = jnp.dot(ks_ref[:, lane : lane + 256], widen(columns, h), preferred_element_type=jnp.float32)
        scores = jnp.where(allowed, scores, NEG)
        top, total, out = finish(scores, vs_ref[h * HD : (h + 1) * HD, :])
        osuf_ref[h * HD : (h + 1) * HD, :] = out
        ssuf_ref[h : h + 1, :] = top
        ssuf_ref[HEADS + h : HEADS + h + 1, :] = total


def attend(qa, k2, v2, gk, gv, cosine, sine, bias, offset):
    f32, bf = jnp.float32, jnp.bfloat16
    return pl.pallas_call(
        attend_kernel,
        out_shape=(
            jax.ShapeDtypeStruct((NX, CH, TOK), bf),
            jax.ShapeDtypeStruct((NX, 2 * HEADS, TOK), f32),
            jax.ShapeDtypeStruct((CH, TOK), f32),
            jax.ShapeDtypeStruct((2 * HEADS, TOK), f32),
            jax.ShapeDtypeStruct((TOK, CH), bf),
        ),
        in_specs=[pl.BlockSpec(memory_space=VMEM)] * 9,
        out_specs=[pl.BlockSpec(memory_space=VMEM)] * 5,
        scratch_shapes=[
            VMEM((CH, KEYS), bf),
            VMEM((CH, 2 * TOK), bf),
            VMEM((2 * TOK, CH), bf),
        ],
        name="attend",
    )(qa, k2, v2, gk, gv, cosine, sine, bias, offset)


def merge_kernel(
    o_ref, stat_ref, osuf_ref, ssuf_ref, out_ref,
    ro_ref, rs_ref, c_ref, o_send, o_recv, t_send, t_recv, a_send, a_recv, loc,
):
    s, t, x, y, z = where_am_i()
    col = s % COL
    tps = [(s, (t + j) % NT) for j in range(1, NT)]
    there = [(x + j) % NX for j in range(1, NX)]
    xs = [(w * COL + col, t) for w in there]
    greet(tps + xs)
    copies = []
    for j in range(NX - 1):
        copies.append(remote(stat_ref.at[there[j]], rs_ref.at[j], t_send.at[j], t_recv.at[j], xs[j]))
        copies.append(remote(o_ref.at[there[j]], ro_ref.at[j], o_send.at[j], o_recv.at[j], xs[j]))
    for copy in copies:
        copy.start()
    for copy in copies:
        copy.wait_recv()
    stats = [ssuf_ref[...], stat_ref[x]] + [rs_ref[j] for j in range(NX - 1)]
    top = stats[0][:HEADS]
    for st in stats[1:]:
        top = jnp.maximum(top, st[:HEADS])
    scales = [jnp.exp2((st[:HEADS] - top) * EXP_SCALE) * st[HEADS:] for st in stats]
    total = scales[0] + scales[1] + scales[2] + scales[3] + scales[4]
    scales = [sc / total for sc in scales]
    heads = []
    for h in range(HEADS):
        part = slice(h * HD, (h + 1) * HD)
        acc = osuf_ref[part, :] * scales[0][h : h + 1]
        acc += o_ref[x, part, :].astype(jnp.float32) * scales[1][h : h + 1]
        for j in range(NX - 1):
            acc += ro_ref[j, part, :].astype(jnp.float32) * scales[2 + j][h : h + 1]
        heads.append(acc)
    c_ref[...] = jnp.concatenate(heads, axis=0).T.astype(jnp.bfloat16)

    def rows(index):
        return c_ref.at[pl.ds(pl.multiple_of(index * PART, PART), PART), :]

    place = out_ref.at[:, pl.ds(pl.multiple_of(t * CH, 128), CH)]
    back = [remote(rows(tps[j][1]), place, a_send.at[j], a_recv.at[j], tps[j]) for j in range(NT - 1)]
    for copy in back:
        copy.start()
    mine = pltpu.make_async_copy(rows(t), place, loc.at[0])
    mine.start()
    mine.wait()
    for copy in back:
        copy.wait_recv()
    for copy in copies + back:
        copy.wait_send()


def merge(o, stat, osuf, ssuf):
    dma = pltpu.SemaphoreType.DMA
    return pl.pallas_call(
        merge_kernel,
        out_shape=jax.ShapeDtypeStruct((PART, NT * CH), jnp.bfloat16),
        in_specs=[pl.BlockSpec(memory_space=VMEM)] * 4,
        out_specs=pl.BlockSpec(memory_space=VMEM),
        scratch_shapes=[
            VMEM((NX - 1, CH, TOK), jnp.bfloat16),
            VMEM((NX - 1, 2 * HEADS, TOK), jnp.float32),
            VMEM((TOK, CH), jnp.bfloat16),
            dma((NX - 1,)), dma((NX - 1,)),
            dma((NX - 1,)), dma((NX - 1,)),
            dma((NT - 1,)), dma((NT - 1,)),
            dma((1,)),
        ],
        compiler_params=pltpu.CompilerParams(collective_id=1, has_side_effects=True),
        name="merge",
    )(o, stat, osuf, ssuf)


def tables(page_table, lengths, group_of):
    s = lax.axis_index("seq")
    x, col = s // COL, s % COL
    blocks = jnp.concatenate([jnp.stack([s - 1, s]), jnp.arange(NX, dtype=jnp.int32) * COL + col])
    rows = (blocks[:, None] * TOK + jnp.arange(TOK, dtype=jnp.int32)[None, :]).astype(jnp.int32)
    starts = (jnp.cumsum(lengths) - lengths).astype(jnp.int32)
    begun = starts[:, None, None] <= rows[None]
    first = jnp.max(jnp.where(begun, starts[:, None, None], 0), axis=0)
    ids = jnp.arange(lengths.shape[0], dtype=jnp.int32)
    request = jnp.sum(begun.astype(jnp.int32), axis=0) - 1
    group = jnp.sum(jnp.where(request[None] == ids[:, None, None], group_of[:, None, None], 0), axis=0)
    offset = rows - first
    position = (COL * NX * PAGE // 2 + offset).astype(jnp.float32)
    inverse_freq = 10000.0 ** (-(jnp.arange(HALF, dtype=jnp.float32) * 2.0 / ROT))
    angles = position[:, None, :] * inverse_freq[None, :, None]
    cosine, sine = jnp.cos(angles), jnp.sin(angles)
    slots = x * COL + jnp.arange(COL, dtype=jnp.int32)
    late = page_table[page_table.shape[0] // 2 :]
    slot_group = jnp.any(slots[:, None] == late[None, :], axis=1).astype(jnp.int32)
    bias = jnp.where(group[2:, None, :] == slot_group[None, :, None], 0.0, NEG).astype(jnp.float32)
    return (
        jnp.concatenate([cosine, cosine], axis=1),
        jnp.concatenate([-sine, sine], axis=1),
        bias,
        offset[1][None, :],
    )


def local(queries, keys, values, pool_keys, pool_values, page_table, lengths, group_of):
    cosine, sine, bias, offset = tables(page_table, lengths, group_of)
    qa, k2, v2, gk, gv = spread(queries, keys, values, pool_keys, pool_values)
    o, stat, osuf, ssuf, new_keys = attend(
        qa, k2, v2, gk.reshape(KEYS, CH), gv.reshape(KEYS, CH), cosine, sine, bias, offset
    )
    context = merge(o, stat, osuf, ssuf)
    return context, new_keys, v2[1]


def solution(mesh):
    return jax.shard_map(
        local,
        mesh=mesh,
        in_specs=(
            P(("seq", "tp"), None),
            P(("seq", "tp"), None),
            P(("seq", "tp"), None),
            P("seq", None, "tp"),
            P("seq", None, "tp"),
            P(),
            P(),
            P(),
        ),
        out_specs=(P(("seq", "tp"), None), P("seq", "tp"), P("seq", "tp")),
        check_vma=False,
    )
```

time: 727 us -> 125 us (0.17)
  the two profiles are of different devices: /device:TPU:1 before, /device:TPU:121 now
where the time goes in v1:
time: 125 us
  Pallas kernels  115 us (92%)
  other arithmetic  4.94 us (4%)
  local copies, waits for them, and re-layouts  4.36 us (3%)
    pallas_call x1, Pallas kernels, spread(): pl.pallas_call(spread_kernel, out_shape=(jax.ShapeDtypeStruct((NX, TOK, C...  60.6 us
    pallas_call x1, Pallas kernels, merge(): pl.pallas_call(merge_kernel, out_shape=jax.ShapeDtypeStruct((PART, NT * C...  28.2 us
    pallas_call x1, Pallas kernels, attend(): pl.pallas_call(attend_kernel, out_shape=(jax.ShapeDtypeStruct((NX, CH, TO...  26.3 us

profile of v1, /device:TPU:121, one launch (start us, length us, event | category | flops | bytes accessed | tf_op | source)
XLA Modules:
  0.0 125.2 jit_solution(13240878226456821212)
XLA Ops:
  0.7 0.1 add_multiply_fusion
  0.7 0.7 slice.13
  1.5 0.2 compare_reduce_fusion
  1.7 0.1 iota_add_fusion
  1.8 0.8 copy.13
  2.5 0.2 reduce-window.9
  2.7 0.1 reduce
  2.8 0.7 sub.22
  3.5 0.2 fusion.1
  3.7 0.1 add_convert_fusion
  3.8 0.5 slice.17.offset_ref
  4.3 0.8 select_reduce_fusion
  5.2 0.7 compare_select_fusion.1.bias_ref
  5.9 0.4 fusion.2
  6.3 0.7 pad_maximum_fusion.1.sin_ref
  7.0 0.7 pad_maximum_fusion.cos_ref
  7.7 60.6 %spread.1 = (bf16[4,256,384]{2,1,0:T(8,128)(2,1)}, bf16[2,256,384]{2,1,0:T(8,128)(2,1)}, bf16[2,256,384]{2,1,0:T(8,128)(2,1)}, bf16[8,2,128,384]{3,2,1,0:T(8,128)(2,1)}, bf16[8,2,128,384]{3,2,1,0:T(8,128)(2,1)}) custom-call(bf16[32,3072]{1,0:T(8,128)(2,1)} %q_ref.1, bf16[32,3072]{1,0:T(8,128)(2,1)} %k_ref.1, bf16[32,3072]{1,0:T(8,128)(2,1)} %v_ref.1, ...), custom_call_target="tpu_custom_call" | custom-call | tf_op jit(solution)/shard_map/spread/pallas_call | solution.py:144
  68.3 0.0 copy-start
  68.3 26.3 %attend.1 = (bf16[4,384,256]{2,1,0:T(8,128)(2,1)}, f32[4,8,256]{2,1,0:T(8,128)}, f32[384,256]{1,0:T(8,128)}, f32[8,256]{1,0:T(8,128)}, bf16[256,384]{1,0:T(8,128)(2,1)}) custom-call(bf16[4,256,384]{2,1,0:T(8,128)(2,1)} %get-tuple-element.13.qa_ref, bf16[2,256,384]{2,1,0:T(8,128)(2,1)} %get-tuple-element.14.k2_ref, ...), custom_call_target="tpu_custom_call" | custom-call | tf_op jit(solution)/shard_map/attend/pallas_call | solution.py:246
  94.6 0.0 copy-done
  94.6 0.7 slice_bitcast_fusion
  95.3 28.2 %merge.1 = bf16[32,3072]{1,0:T(8,128)(2,1)} custom-call(bf16[4,384,256]{2,1,0:T(8,128)(2,1)} %get-tuple-element.18.o_ref, f32[4,8,256]{2,1,0:T(8,128)} %get-tuple-element.19.stat_ref, f32[384,256]{1,0:T(8,128)} %get-tuple-element.20.osuf_ref, f32[8,256]{1,0:T(8,128)} %get-tuple-element.21.ssuf_ref), custom_call_target="tpu_custom_call" | custom-call | tf_op jit(solution)/shard_map/merge/pallas_call | solution.py:319
  123.6 1.6 %copy.15 = bf16[32,3072]{1,0:T(8,128)(2,1)} copy(bf16[32,3072]{1,0:T(8,128)(2,1)} %merge.1) | data formatting | bytes 393216
  (5 shorter events, 0.0 us)
Async XLA Ops:
  68.3 26.3 %copy-start = (bf16[2,256,384]{2,1,0:T(8,128)(2,1)S(1)}, bf16[2,256,384]{2,1,0:T(8,128)(2,1)}, u32[]{:S(2)}) copy-start(bf16[2,256,384]{2,1,0:T(8,128)(2,1)} %get-tuple-element.15.v2_ref) | copy-start | bytes 1179652

commit v2 on v1

--- a/solution.py
+++ b/solution.py
@@ -49,18 +49,19 @@
 def spread_kernel(
     q_ref, k_ref, v_ref, pk_ref, pv_ref,
     qa_ref, k2_ref, v2_ref, gk_ref, gv_ref,
-    a_send, a_recv, z_send, z_recv, r_send, r_recv, x_send, x_recv, s_send, s_recv, loc,
+    a_send, a_recv, z_send, z_recv, r_send, r_recv, y_send, y_recv, x_send, x_recv, s_send, s_recv, loc,
 ):
     s, t, x, y, z = where_am_i()
     col = s % COL
     partner = (s + 1 - 2 * z, t)
     up = (x * COL + ((y + 1) % NY) * NZ + z, t)
     down = (x * COL + ((y + NY - 1) % NY) * NZ + z, t)
+    east = (((x + 1) % NX) * COL + col, t)
+    west = (((x + NX - 1) % NX) * COL + col, t)
     after = ((s + 1) % SEQ, t)
     before = ((s + SEQ - 1) % SEQ, t)
     tps = [(s, (t + j) % NT) for j in range(1, NT)]
-    xs = [(((x + j) % NX) * COL + col, t) for j in range(1, NX)]
-    greet([partner, up, down, after, before] + tps + xs)
+    greet([partner, up, down, east, west, after, before] + tps)
 
     pending = []
 
@@ -69,8 +70,9 @@
         pending.append(copy)
         return copy
 
+    low, high = pl.ds(0, PAGE // 2), pl.ds(PAGE // 2, PAGE // 2)
     zk = go(remote(pk_ref.at[0], gk_ref.at[y, z], z_send.at[0], z_recv.at[0], partner))
-    zv = go(remote(pv_ref.at[0], gv_ref.at[y, z], z_send.at[1], z_recv.at[1], partner))
+    zv = go(remote(pv_ref.at[0, low], gv_ref.at[y, z, low], z_send.at[1], z_recv.at[1], partner))
 
     def rows(ref, kind):
         return ref.at[x if kind == 0 else 1, pl.ds(pl.multiple_of(t * PART, PART), PART), :]
@@ -79,14 +81,6 @@
         return ref.at[:, pl.ds(pl.multiple_of(index * CH, 128), CH)]
 
     kinds = [(q_ref, qa_ref), (k_ref, k2_ref), (v_ref, v2_ref)]
-    swaps = []
-    for kind, (src, dst) in enumerate(kinds):
-        swaps.append(
-            [
-                go(remote(lanes(src, tps[j][1]), rows(dst, kind), a_send.at[kind, j], a_recv.at[kind, j], tps[j]))
-                for j in range(NT - 1)
-            ]
-        )
     own = [
         pltpu.make_async_copy(pk_ref.at[0], gk_ref.at[y, z], loc.at[0]),
         pltpu.make_async_copy(pv_ref.at[0], gv_ref.at[y, z], loc.at[1]),
@@ -96,34 +90,66 @@
     ]
     for copy in own:
         copy.start()
+    swaps = []
+    for kind, (src, dst) in enumerate(kinds):
+        swaps.append(
+            [
+                go(remote(lanes(src, tps[j][1]), rows(dst, kind), a_send.at[kind, j], a_recv.at[kind, j], tps[j]))
+                for j in range(NT - 1)
+            ]
+        )
     for copy in own:
         copy.wait()
-    zk.wait_recv()
-    zv.wait_recv()
 
     flows = [(gk_ref, 0, 4), (gv_ref, 0, 3), (gk_ref, 1, 3), (gv_ref, 1, 4)]
     last = [None] * len(flows)
+    single = [None, None]
+    handed = []
+
+    def index_of(way, step):
+        return (y + NY - step) % NY if way == 0 else (y + step) % NY
+
+    def hop_single(step):
+        for way, hops in ((0, 4), (1, 3)):
+            block = gv_ref.at[index_of(way, step), z, high]
+            if single[way] is not None:
+                single[way].wait_recv()
+                single[way] = None
+            if step < hops:
+                single[way] = go(
+                    remote(block, block, y_send.at[way, step], y_recv.at[way, step], up if way == 0 else down)
+                )
+            if step <= hops and (way == 0 or step > 0):
+                handed.append(go(remote(block, block, y_send.at[2 + way, step], y_recv.at[2 + way, step], partner)))
 
     def hop(step):
+        hop_single(step)
+        if step == 0:
+            zk.wait_recv()
+            zv.wait_recv()
         for index, (ref, way, hops) in enumerate(flows):
-            if step > 0 and last[index] is not None:
+            if last[index] is not None:
                 last[index].wait_recv()
                 last[index] = None
             if step < hops:
-                at = (y + NY - step) % NY if way == 0 else (y + step) % NY
+                at = index_of(way, step)
+                block = ref.at[at] if ref is gk_ref else ref.at[at, :, low]
                 last[index] = go(
-                    remote(
-                        ref.at[at], ref.at[at], r_send.at[index, step], r_recv.at[index, step], up if way == 0 else down
-                    )
+                    remote(block, block, r_send.at[index, step], r_recv.at[index, step], up if way == 0 else down)
                 )
 
     hop(0)
     for copy in swaps[0]:
         copy.wait_recv()
     across = [
-        go(remote(qa_ref.at[x], qa_ref.at[x], x_send.at[j], x_recv.at[j], xs[j])) for j in range(NX - 1)
+        go(remote(qa_ref.at[x], qa_ref.at[x], x_send.at[i], x_recv.at[i], to)) for i, to in enumerate((east, west))
     ]
     hop(1)
+    relays = []
+    for i, to in enumerate((east, west)):
+        across[i].wait_recv()
+        half = qa_ref.at[(x + NX - 1) % NX if i == 0 else (x + 1) % NX, pl.ds(i * (TOK // 2), TOK // 2), :]
+        relays.append(go(remote(half, half, x_send.at[2 + i], x_recv.at[2 + i], to)))
     for copy in swaps[1] + swaps[2]:
         copy.wait_recv()
     shifts = [
@@ -132,7 +158,7 @@
     hop(2)
     hop(3)
     hop(4)
-    for copy in across + shifts:
+    for copy in relays + shifts + handed:
         copy.wait_recv()
     for copy in pending:
         copy.wait_send()
@@ -156,7 +182,8 @@
             dma((3, NT - 1)), dma((3, NT - 1)),
             dma((2,)), dma((2,)),
             dma((4, 4)), dma((4, 4)),
-            dma((NX - 1,)), dma((NX - 1,)),
+            dma((4, 5)), dma((4, 5)),
+            dma((4,)), dma((4,)),
             dma((2,)), dma((2,)),
             dma((5,)),
         ],
@@ -187,10 +214,18 @@
 
 def attend_kernel(
     qa_ref, k2_ref, v2_ref, gk_ref, gv_ref, cos_ref, sin_ref, bias_ref, offset_ref,
-    o_ref, stat_ref, osuf_ref, ssuf_ref, newk_ref,
-    vt_ref, vs_ref, ks_ref,
+    out_ref, newk_ref,
+    vt_ref, vs_ref, ks_ref, o_ref, stat_ref, ro_ref, rs_ref, c_ref,
+    o_send, o_recv, t_send, t_recv, a_send, a_recv, loc,
 ):
-    me = lax.axis_index("seq") // COL
+    s, t, x, y, z = where_am_i()
+    col = s % COL
+    tps = [(s, (t + j) % NT) for j in range(1, NT)]
+    peers = tps + [(((x + j) % NX) * COL + col, t) for j in range(1, NX)]
+    barrier = pltpu.get_barrier_semaphore()
+    for peer in peers:
+        pl.semaphore_signal(barrier, inc=1, device_id=peer, device_id_type=MESH)
+
     for b in range(2):
         turned = turn(k2_ref[b].astype(jnp.float32).T, cos_ref[b], sin_ref[b])
         turned = turned.T.astype(jnp.bfloat16)
@@ -201,6 +236,7 @@
         vt_ref[:, b * 256 : (b + 1) * 256] = (
             gv_ref[b * 256 : (b + 1) * 256, :].astype(jnp.float32).T.astype(jnp.bfloat16)
         )
+    pl.semaphore_wait(barrier, len(peers))
 
     def queries(b):
         return turn(qa_ref[b].astype(jnp.float32).T, cos_ref[2 + b], sin_ref[2 + b]).astype(jnp.bfloat16)
@@ -212,7 +248,16 @@
         summed = jnp.dot(values, weights.astype(jnp.bfloat16), preferred_element_type=jnp.float32)
         return top, total, summed / total
 
-    def one_block(b, carry):
+    def hand_over(j):
+        b = (x + NX - 1 - j) % NX
+        to = (b * COL + col, t)
+        return [
+            remote(stat_ref.at[b], rs_ref.at[j], t_send.at[j], t_recv.at[j], to),
+            remote(o_ref.at[b], ro_ref.at[j], o_send.at[j], o_recv.at[j], to),
+        ]
+
+    def one_block(j, carry):
+        b = (x + NX - 1 - j) % NX
         columns = queries(b)
         bias = bias_ref[b]
         for h in range(HEADS):
@@ -223,78 +268,46 @@
             o_ref[b, h * HD : (h + 1) * HD, :] = out.astype(jnp.bfloat16)
             stat_ref[b, h : h + 1, :] = top
             stat_ref[b, HEADS + h : HEADS + h + 1, :] = total
+            if h == 0:
+
+                @pl.when(j > 0)
+                def _():
+                    for copy in hand_over(j - 1):
+                        copy.start()
+
         return carry
 
     lax.fori_loop(0, NX, one_block, 0)
 
-    columns = queries(me)
+    columns = queries(x)
     token = lax.broadcasted_iota(jnp.int32, (2 * TOK, TOK), 1) + TOK
     key = lax.broadcasted_iota(jnp.int32, (2 * TOK, TOK), 0)
     allowed = (key <= token) & (key >= token - offset_ref[...])
+    suffix = []
     for h in range(HEADS):
         lane = (h // 2) * 128
         scores = jnp.dot(ks_ref[:, lane : lane + 256], widen(columns, h), preferred_element_type=jnp.float32)
         scores = jnp.where(allowed, scores, NEG)
-        top, total, out = finish(scores, vs_ref[h * HD : (h + 1) * HD, :])
-        osuf_ref[h * HD : (h + 1) * HD, :] = out
-        ssuf_ref[h : h + 1, :] = top
-        ssuf_ref[HEADS + h : HEADS + h + 1, :] = total
-
-
-def attend(qa, k2, v2, gk, gv, cosine, sine, bias, offset):
-    f32, bf = jnp.float32, jnp.bfloat16
-    return pl.pallas_call(
-        attend_kernel,
-        out_shape=(
-            jax.ShapeDtypeStruct((NX, CH, TOK), bf),
-            jax.ShapeDtypeStruct((NX, 2 * HEADS, TOK), f32),
-            jax.ShapeDtypeStruct((CH, TOK), f32),
-            jax.ShapeDtypeStruct((2 * HEADS, TOK), f32),
-            jax.ShapeDtypeStruct((TOK, CH), bf),
-        ),
-        in_specs=[pl.BlockSpec(memory_space=VMEM)] * 9,
-        out_specs=[pl.BlockSpec(memory_space=VMEM)] * 5,
-        scratch_shapes=[
-            VMEM((CH, KEYS), bf),
-            VMEM((CH, 2 * TOK), bf),
-            VMEM((2 * TOK, CH), bf),
-        ],
-        name="attend",
-    )(qa, k2, v2, gk, gv, cosine, sine, bias, offset)
-
-
-def merge_kernel(
-    o_ref, stat_ref, osuf_ref, ssuf_ref, out_ref,
-    ro_ref, rs_ref, c_ref, o_send, o_recv, t_send, t_recv, a_send, a_recv, loc,
-):
-    s, t, x, y, z = where_am_i()
-    col = s % COL
-    tps = [(s, (t + j) % NT) for j in range(1, NT)]
-    there = [(x + j) % NX for j in range(1, NX)]
-    xs = [(w * COL + col, t) for w in there]
-    greet(tps + xs)
-    copies = []
-    for j in range(NX - 1):
-        copies.append(remote(stat_ref.at[there[j]], rs_ref.at[j], t_send.at[j], t_recv.at[j], xs[j]))
-        copies.append(remote(o_ref.at[there[j]], ro_ref.at[j], o_send.at[j], o_recv.at[j], xs[j]))
-    for copy in copies:
-        copy.start()
+        suffix.append(finish(scores, vs_ref[h * HD : (h + 1) * HD, :]))
+
+    copies = [copy for j in range(NX - 1) for copy in hand_over(j)]
     for copy in copies:
         copy.wait_recv()
-    stats = [ssuf_ref[...], stat_ref[x]] + [rs_ref[j] for j in range(NX - 1)]
-    top = stats[0][:HEADS]
-    for st in stats[1:]:
-        top = jnp.maximum(top, st[:HEADS])
-    scales = [jnp.exp2((st[:HEADS] - top) * EXP_SCALE) * st[HEADS:] for st in stats]
-    total = scales[0] + scales[1] + scales[2] + scales[3] + scales[4]
-    scales = [sc / total for sc in scales]
     heads = []
     for h in range(HEADS):
         part = slice(h * HD, (h + 1) * HD)
-        acc = osuf_ref[part, :] * scales[0][h : h + 1]
-        acc += o_ref[x, part, :].astype(jnp.float32) * scales[1][h : h + 1]
-        for j in range(NX - 1):
-            acc += ro_ref[j, part, :].astype(jnp.float32) * scales[2 + j][h : h + 1]
+        one, two = slice(h, h + 1), slice(HEADS + h, HEADS + h + 1)
+        tops = [suffix[h][0], stat_ref[x, one, :]] + [rs_ref[j, one, :] for j in range(NX - 1)]
+        totals = [suffix[h][1], stat_ref[x, two, :]] + [rs_ref[j, two, :] for j in range(NX - 1)]
+        outs = [suffix[h][2], o_ref[x, part, :]] + [ro_ref[j, part, :] for j in range(NX - 1)]
+        top = tops[0]
+        for other in tops[1:]:
+            top = jnp.maximum(top, other)
+        scales = [jnp.exp2((a - top) * EXP_SCALE) * b for a, b in zip(tops, totals)]
+        total = scales[0] + scales[1] + scales[2] + scales[3] + scales[4]
+        acc = outs[0] * (scales[0] / total)
+        for out, scale in zip(outs[1:], scales[1:]):
+            acc += out.astype(jnp.float32) * (scale / total)
         heads.append(acc)
     c_ref[...] = jnp.concatenate(heads, axis=0).T.astype(jnp.bfloat16)
 
@@ -314,25 +327,34 @@
         copy.wait_send()
 
 
-def merge(o, stat, osuf, ssuf):
+def attend(qa, k2, v2, gk, gv, cosine, sine, bias, offset):
+    f32, bf = jnp.float32, jnp.bfloat16
     dma = pltpu.SemaphoreType.DMA
     return pl.pallas_call(
-        merge_kernel,
-        out_shape=jax.ShapeDtypeStruct((PART, NT * CH), jnp.bfloat16),
-        in_specs=[pl.BlockSpec(memory_space=VMEM)] * 4,
-        out_specs=pl.BlockSpec(memory_space=VMEM),
+        attend_kernel,
+        out_shape=(
+            jax.ShapeDtypeStruct((PART, NT * CH), bf),
+            jax.ShapeDtypeStruct((TOK, CH), bf),
+        ),
+        in_specs=[pl.BlockSpec(memory_space=VMEM)] * 9,
+        out_specs=[pl.BlockSpec(memory_space=VMEM)] * 2,
         scratch_shapes=[
-            VMEM((NX - 1, CH, TOK), jnp.bfloat16),
-            VMEM((NX - 1, 2 * HEADS, TOK), jnp.float32),
-            VMEM((TOK, CH), jnp.bfloat16),
+            VMEM((CH, KEYS), bf),
+            VMEM((CH, 2 * TOK), bf),
+            VMEM((2 * TOK, CH), bf),
+            VMEM((NX, CH, TOK), bf),
+            VMEM((NX, 2 * HEADS, TOK), f32),
+            VMEM((NX - 1, CH, TOK), bf),
+            VMEM((NX - 1, 2 * HEADS, TOK), f32),
+            VMEM((TOK, CH), bf),
             dma((NX - 1,)), dma((NX - 1,)),
             dma((NX - 1,)), dma((NX - 1,)),
             dma((NT - 1,)), dma((NT - 1,)),
             dma((1,)),
         ],
         compiler_params=pltpu.CompilerParams(collective_id=1, has_side_effects=True),
-        name="merge",
-    )(o, stat, osuf, ssuf)
+        name="attend",
+    )(qa, k2, v2, gk, gv, cosine, sine, bias, offset)
 
 
 def tables(page_table, lengths, group_of):
@@ -366,10 +388,9 @@
 def local(queries, keys, values, pool_keys, pool_values, page_table, lengths, group_of):
     cosine, sine, bias, offset = tables(page_table, lengths, group_of)
     qa, k2, v2, gk, gv = spread(queries, keys, values, pool_keys, pool_values)
-    o, stat, osuf, ssuf, new_keys = attend(
+    context, new_keys = attend(
         qa, k2, v2, gk.reshape(KEYS, CH), gv.reshape(KEYS, CH), cosine, sine, bias, offset
     )
-    context = merge(o, stat, osuf, ssuf)
     return context, new_keys, v2[1]
 
 

time: 125 us -> 114 us (0.912)
  the two profiles are of different devices: /device:TPU:121 before, /device:TPU:1 now
where the time goes in v2:
time: 114 us
  Pallas kernels  102 us (89%)
  local copies, waits for them, and re-layouts  5.98 us (5%)
  other arithmetic  4.95 us (4%)
    pallas_call x1, Pallas kernels, spread(): pl.pallas_call(spread_kernel, out_shape=(jax.ShapeDtypeStruct((NX, TOK, C...  60 us
    pallas_call x1, Pallas kernels, attend(): pl.pallas_call(attend_kernel, out_shape=(jax.ShapeDtypeStruct((PART, NT *...  42.4 us
    unnamed x4, local copies, waits for them, and re-layouts  3.24 us

profile of v2, /device:TPU:1, one launch (start us, length us, event | category | flops | bytes accessed | tf_op | source)
XLA Modules:
  0.0 114.1 jit_solution(15474418753356667911)
XLA Ops:
  0.7 0.1 add_multiply_fusion
  0.7 0.7 slice.13
  1.5 0.2 compare_reduce_fusion
  1.7 0.1 iota_add_fusion
  1.8 0.8 copy.13
  2.5 0.2 reduce-window.9
  2.7 0.1 reduce
  2.8 0.7 sub.22
  3.5 0.2 fusion.1
  3.7 0.1 add_convert_fusion
  3.8 0.5 slice.17.offset_ref
  4.3 0.8 select_reduce_fusion
  5.2 0.7 compare_select_fusion.1.bias_ref
  5.9 0.4 fusion.2
  6.3 0.7 pad_maximum_fusion.1.sin_ref
  7.0 0.7 pad_maximum_fusion.cos_ref
  7.7 60.0 %spread.1 = (bf16[4,256,384]{2,1,0:T(8,128)(2,1)}, bf16[2,256,384]{2,1,0:T(8,128)(2,1)}, bf16[2,256,384]{2,1,0:T(8,128)(2,1)}, bf16[8,2,128,384]{3,2,1,0:T(8,128)(2,1)}, bf16[8,2,128,384]{3,2,1,0:T(8,128)(2,1)}) custom-call(bf16[32,3072]{1,0:T(8,128)(2,1)} %q_ref.1, bf16[32,3072]{1,0:T(8,128)(2,1)} %k_ref.1, bf16[32,3072]{1,0:T(8,128)(2,1)} %v_ref.1, ...), custom_call_target="tpu_custom_call" | custom-call | tf_op jit(solution)/shard_map/spread/pallas_call | solution.py:170
  67.7 0.0 copy-start
  67.7 42.4 %attend.1 = (bf16[32,3072]{1,0:T(8,128)(2,1)}, bf16[256,384]{1,0:T(8,128)(2,1)}) custom-call(bf16[4,256,384]{2,1,0:T(8,128)(2,1)} %get-tuple-element.10.qa_ref, bf16[2,256,384]{2,1,0:T(8,128)(2,1)} %get-tuple-element.11.k2_ref, bf16[2,256,384]{2,1,0:T(8,128)(2,1)} %get-tuple-element.12.v2_ref, bf16[2048,384]{1,0:T(8,128)(2,1)} %bitcast.7, ...), custom_call_target="tpu_custom_call" | custom-call | tf_op jit(solution)/shard_map/attend/pallas_call | solution.py:333
  110.1 0.0 copy-done
  110.1 0.7 slice_bitcast_fusion
  110.8 1.6 %copy.16 = bf16[32,3072]{1,0:T(8,128)(2,1)} copy(bf16[32,3072]{1,0:T(8,128)(2,1)} %get-tuple-element.28) | data formatting | bytes 393216
  112.4 1.6 %copy.17 = bf16[256,384]{1,0:T(8,128)(2,1)} copy(bf16[256,384]{1,0:T(8,128)(2,1)} %get-tuple-element.29) | data formatting | bytes 393216
  (5 shorter events, 0.0 us)
Async XLA Ops:
  67.7 42.5 %copy-start = (bf16[2,256,384]{2,1,0:T(8,128)(2,1)S(1)}, bf16[2,256,384]{2,1,0:T(8,128)(2,1)}, u32[]{:S(2)}) copy-start(bf16[2,256,384]{2,1,0:T(8,128)(2,1)} %get-tuple-element.12.v2_ref) | copy-start | bytes 1179652

commit v3 on v2

--- a/solution.py
+++ b/solution.py
@@ -46,10 +46,33 @@
     )
 
 
-def spread_kernel(
-    q_ref, k_ref, v_ref, pk_ref, pv_ref,
+def turn(matrix, cosine, sine):
+    parts = []
+    for h in range(HEADS):
+        lead = matrix[h * HD : h * HD + ROT]
+        other = jnp.concatenate([lead[HALF:], lead[:HALF]], axis=0)
+        parts += [lead * cosine + other * sine, matrix[h * HD + ROT : (h + 1) * HD]]
+    return jnp.concatenate(parts, axis=0)
+
+
+def widen(columns, h):
+    start = h * HD - (h // 2) * 128
+    pieces = []
+    if start:
+        pieces.append(jnp.zeros((start, TOK), jnp.bfloat16))
+    pieces.append(columns[h * HD : (h + 1) * HD])
+    if start + HD < 256:
+        pieces.append(jnp.zeros((256 - start - HD, TOK), jnp.bfloat16))
+    return jnp.concatenate(pieces, axis=0)
+
+
+def attend_kernel(
+    q_ref, k_ref, v_ref, pk_ref, pv_ref, cos_ref, sin_ref, bias_ref, offset_ref,
+    out_ref, newk_ref, newv_ref,
     qa_ref, k2_ref, v2_ref, gk_ref, gv_ref,
-    a_send, a_recv, z_send, z_recv, r_send, r_recv, y_send, y_recv, x_send, x_recv, s_send, s_recv, loc,
+    qt_ref, vt_ref, vs_ref, ks_ref, acc_ref, run_ref, o_ref, stat_ref, ro_ref, rs_ref, c_ref,
+    a_send, a_recv, z_send, z_recv, r_send, r_recv, y_send, y_recv, x_send, x_recv, s_send, s_recv,
+    o_send, o_recv, t_send, t_recv, b_send, b_recv, loc,
 ):
     s, t, x, y, z = where_am_i()
     col = s % COL
@@ -58,10 +81,11 @@
     down = (x * COL + ((y + NY - 1) % NY) * NZ + z, t)
     east = (((x + 1) % NX) * COL + col, t)
     west = (((x + NX - 1) % NX) * COL + col, t)
+    across_x = (((x + 2) % NX) * COL + col, t)
     after = ((s + 1) % SEQ, t)
     before = ((s + SEQ - 1) % SEQ, t)
     tps = [(s, (t + j) % NT) for j in range(1, NT)]
-    greet([partner, up, down, east, west, after, before] + tps)
+    greet([partner, up, down, east, west, across_x, after, before] + tps)
 
     pending = []
 
@@ -104,7 +128,7 @@
     flows = [(gk_ref, 0, 4), (gv_ref, 0, 3), (gk_ref, 1, 3), (gv_ref, 1, 4)]
     last = [None] * len(flows)
     single = [None, None]
-    handed = []
+    handed = {}
 
     def index_of(way, step):
         return (y + NY - step) % NY if way == 0 else (y + step) % NY
@@ -120,7 +144,9 @@
                     remote(block, block, y_send.at[way, step], y_recv.at[way, step], up if way == 0 else down)
                 )
             if step <= hops and (way == 0 or step > 0):
-                handed.append(go(remote(block, block, y_send.at[2 + way, step], y_recv.at[2 + way, step], partner)))
+                handed.setdefault(step, []).append(
+                    go(remote(block, block, y_send.at[2 + way, step], y_recv.at[2 + way, step], partner))
+                )
 
     def hop(step):
         hop_single(step)
@@ -138,12 +164,73 @@
                     remote(block, block, r_send.at[index, step], r_recv.at[index, step], up if way == 0 else down)
                 )
 
+    def prepare(b):
+        turned = turn(qa_ref[b].astype(jnp.float32).T, cos_ref[2 + b], sin_ref[2 + b])
+        qt_ref[b] = turned.astype(jnp.bfloat16)
+
+    def receive_values(step, places):
+        for copy in handed.pop(step, []):
+            copy.wait_recv()
+        for at in places:
+            vt_ref[at] = gv_ref[at].reshape(NZ * PAGE, CH).astype(jnp.float32).T.astype(jnp.bfloat16)
+
+    def score(b, h, at):
+        lane = (h // 2) * 128
+        keys = gk_ref[at, :, :, lane : lane + 256].reshape(NZ * PAGE, 256)
+        scores = jnp.dot(keys, widen(qt_ref[b], h), preferred_element_type=jnp.float32)
+        return (scores.reshape(NZ, PAGE, TOK) + bias_ref[b, at][:, None, :]).reshape(NZ * PAGE, TOK)
+
+    def weigh(scores, top, values):
+        total, summed = None, None
+        for block, value in zip(scores, values):
+            weights = jnp.exp2((block - top) * EXP_SCALE)
+            part = jnp.sum(weights, axis=0, keepdims=True)
+            out = jnp.dot(value, weights.astype(jnp.bfloat16), preferred_element_type=jnp.float32)
+            total = part if total is None else total + part
+            summed = out if summed is None else summed + out
+        return total, summed
+
+    def peak(scores):
+        top = jnp.max(scores[0], axis=0, keepdims=True)
+        for block in scores[1:]:
+            top = jnp.maximum(top, jnp.max(block, axis=0, keepdims=True))
+        return top
+
+    def update(b, h, places, first):
+        part = slice(h * HD, (h + 1) * HD)
+        scores = [score(b, h, at) for at in places]
+        top = peak(scores)
+        if not first:
+            old = run_ref[b, h : h + 1, :]
+            top = jnp.maximum(old, top)
+        total, summed = weigh(scores, top, [vt_ref[at, part, :] for at in places])
+        if not first:
+            factor = jnp.exp2((old - top) * EXP_SCALE)
+            total += run_ref[b, HEADS + h : HEADS + h + 1, :] * factor
+            summed += acc_ref[b, part, :] * factor
+        return top, total, summed
+
+    def absorb(places, first=False):
+        def one(b, carry):
+            for h in range(HEADS):
+                top, total, summed = update(b, h, places, first)
+                run_ref[b, h : h + 1, :] = top
+                run_ref[b, HEADS + h : HEADS + h + 1, :] = total
+                acc_ref[b, h * HD : (h + 1) * HD, :] = summed
+            return carry
+
+        lax.fori_loop(0, NX, one, 0)
+
+    def ahead(n):
+        return (y + n) % NY
+
     hop(0)
     for copy in swaps[0]:
         copy.wait_recv()
     across = [
         go(remote(qa_ref.at[x], qa_ref.at[x], x_send.at[i], x_recv.at[i], to)) for i, to in enumerate((east, west))
     ]
+    prepare(x)
     hop(1)
     relays = []
     for i, to in enumerate((east, west)):
@@ -155,98 +242,25 @@
     shifts = [
         go(remote(ref.at[1], ref.at[0], s_send.at[i], s_recv.at[i], after)) for i, ref in enumerate((k2_ref, v2_ref))
     ]
+    newv_ref[...] = v2_ref[1]
+    prepare((x + 1) % NX)
+    prepare((x + 3) % NX)
+    receive_values(0, [y])
+    receive_values(1, [ahead(1), ahead(7)])
+    for copy in relays:
+        copy.wait_recv()
+    prepare((x + 2) % NX)
+    absorb([y], True)
     hop(2)
+    absorb([ahead(1), ahead(7)])
+    receive_values(2, [ahead(2), ahead(6)])
+    absorb([ahead(2)])
     hop(3)
+    absorb([ahead(6)])
+    receive_values(3, [ahead(3), ahead(5)])
+    absorb([ahead(3), ahead(5)])
     hop(4)
-    for copy in relays + shifts + handed:
-        copy.wait_recv()
-    for copy in pending:
-        copy.wait_send()
-
-
-def spread(q, k, v, pk, pv):
-    bf = jnp.bfloat16
-    dma = pltpu.SemaphoreType.DMA
-    return pl.pallas_call(
-        spread_kernel,
-        out_shape=(
-            jax.ShapeDtypeStruct((NX, TOK, CH), bf),
-            jax.ShapeDtypeStruct((2, TOK, CH), bf),
-            jax.ShapeDtypeStruct((2, TOK, CH), bf),
-            jax.ShapeDtypeStruct((NY, NZ, PAGE, CH), bf),
-            jax.ShapeDtypeStruct((NY, NZ, PAGE, CH), bf),
-        ),
-        in_specs=[pl.BlockSpec(memory_space=VMEM)] * 5,
-        out_specs=[pl.BlockSpec(memory_space=VMEM)] * 5,
-        scratch_shapes=[
-            dma((3, NT - 1)), dma((3, NT - 1)),
-            dma((2,)), dma((2,)),
-            dma((4, 4)), dma((4, 4)),
-            dma((4, 5)), dma((4, 5)),
-            dma((4,)), dma((4,)),
-            dma((2,)), dma((2,)),
-            dma((5,)),
-        ],
-        compiler_params=pltpu.CompilerParams(collective_id=0, has_side_effects=True),
-        name="spread",
-    )(q, k, v, pk, pv)
-
-
-def turn(matrix, cosine, sine):
-    parts = []
-    for h in range(HEADS):
-        lead = matrix[h * HD : h * HD + ROT]
-        other = jnp.concatenate([lead[HALF:], lead[:HALF]], axis=0)
-        parts += [lead * cosine + other * sine, matrix[h * HD + ROT : (h + 1) * HD]]
-    return jnp.concatenate(parts, axis=0)
-
-
-def widen(columns, h):
-    start = h * HD - (h // 2) * 128
-    pieces = []
-    if start:
-        pieces.append(jnp.zeros((start, TOK), jnp.bfloat16))
-    pieces.append(columns[h * HD : (h + 1) * HD])
-    if start + HD < 256:
-        pieces.append(jnp.zeros((256 - start - HD, TOK), jnp.bfloat16))
-    return jnp.concatenate(pieces, axis=0)
-
-
-def attend_kernel(
-    qa_ref, k2_ref, v2_ref, gk_ref, gv_ref, cos_ref, sin_ref, bias_ref, offset_ref,
-    out_ref, newk_ref,
-    vt_ref, vs_ref, ks_ref, o_ref, stat_ref, ro_ref, rs_ref, c_ref,
-    o_send, o_recv, t_send, t_recv, a_send, a_recv, loc,
-):
-    s, t, x, y, z = where_am_i()
-    col = s % COL
-    tps = [(s, (t + j) % NT) for j in range(1, NT)]
-    peers = tps + [(((x + j) % NX) * COL + col, t) for j in range(1, NX)]
-    barrier = pltpu.get_barrier_semaphore()
-    for peer in peers:
-        pl.semaphore_signal(barrier, inc=1, device_id=peer, device_id_type=MESH)
-
-    for b in range(2):
-        turned = turn(k2_ref[b].astype(jnp.float32).T, cos_ref[b], sin_ref[b])
-        turned = turned.T.astype(jnp.bfloat16)
-        ks_ref[b * TOK : (b + 1) * TOK, :] = turned
-        vs_ref[:, b * TOK : (b + 1) * TOK] = v2_ref[b].astype(jnp.float32).T.astype(jnp.bfloat16)
-    newk_ref[...] = ks_ref[TOK:, :]
-    for b in range(KEYS // 256):
-        vt_ref[:, b * 256 : (b + 1) * 256] = (
-            gv_ref[b * 256 : (b + 1) * 256, :].astype(jnp.float32).T.astype(jnp.bfloat16)
-        )
-    pl.semaphore_wait(barrier, len(peers))
-
-    def queries(b):
-        return turn(qa_ref[b].astype(jnp.float32).T, cos_ref[2 + b], sin_ref[2 + b]).astype(jnp.bfloat16)
-
-    def finish(scores, values):
-        top = jnp.max(scores, axis=0, keepdims=True)
-        weights = jnp.exp2((scores - top) * EXP_SCALE)
-        total = jnp.sum(weights, axis=0, keepdims=True)
-        summed = jnp.dot(values, weights.astype(jnp.bfloat16), preferred_element_type=jnp.float32)
-        return top, total, summed / total
+    receive_values(4, [ahead(4)])
 
     def hand_over(j):
         b = (x + NX - 1 - j) % NX
@@ -256,16 +270,11 @@
             remote(o_ref.at[b], ro_ref.at[j], o_send.at[j], o_recv.at[j], to),
         ]
 
-    def one_block(j, carry):
+    def close(j, carry):
         b = (x + NX - 1 - j) % NX
-        columns = queries(b)
-        bias = bias_ref[b]
         for h in range(HEADS):
-            lane = (h // 2) * 128
-            scores = jnp.dot(gk_ref[:, lane : lane + 256], widen(columns, h), preferred_element_type=jnp.float32)
-            scores = (scores.reshape(COL, PAGE, TOK) + bias[:, None, :]).reshape(KEYS, TOK)
-            top, total, out = finish(scores, vt_ref[h * HD : (h + 1) * HD, :])
-            o_ref[b, h * HD : (h + 1) * HD, :] = out.astype(jnp.bfloat16)
+            top, total, summed = update(b, h, [ahead(4)], False)
+            o_ref[b, h * HD : (h + 1) * HD, :] = (summed / total).astype(jnp.bfloat16)
             stat_ref[b, h : h + 1, :] = top
             stat_ref[b, HEADS + h : HEADS + h + 1, :] = total
             if h == 0:
@@ -277,9 +286,16 @@
 
         return carry
 
-    lax.fori_loop(0, NX, one_block, 0)
-
-    columns = queries(x)
+    lax.fori_loop(0, NX, close, 0)
+
+    for copy in shifts:
+        copy.wait_recv()
+    for b in range(2):
+        turned = turn(k2_ref[b].astype(jnp.float32).T, cos_ref[b], sin_ref[b])
+        ks_ref[b * TOK : (b + 1) * TOK, :] = turned.T.astype(jnp.bfloat16)
+        vs_ref[:, b * TOK : (b + 1) * TOK] = v2_ref[b].astype(jnp.float32).T.astype(jnp.bfloat16)
+    newk_ref[...] = ks_ref[TOK:, :]
+    columns = qt_ref[x]
     token = lax.broadcasted_iota(jnp.int32, (2 * TOK, TOK), 1) + TOK
     key = lax.broadcasted_iota(jnp.int32, (2 * TOK, TOK), 0)
     allowed = (key <= token) & (key >= token - offset_ref[...])
@@ -287,8 +303,10 @@
     for h in range(HEADS):
         lane = (h // 2) * 128
         scores = jnp.dot(ks_ref[:, lane : lane + 256], widen(columns, h), preferred_element_type=jnp.float32)
-        scores = jnp.where(allowed, scores, NEG)
-        suffix.append(finish(scores, vs_ref[h * HD : (h + 1) * HD, :]))
+        scores = [jnp.where(allowed, scores, NEG)]
+        top = peak(scores)
+        total, summed = weigh(scores, top, [vs_ref[h * HD : (h + 1) * HD, :]])
+        suffix.append((top, total, summed / total))
 
     copies = [copy for j in range(NX - 1) for copy in hand_over(j)]
     for copy in copies:
@@ -311,23 +329,23 @@
         heads.append(acc)
     c_ref[...] = jnp.concatenate(heads, axis=0).T.astype(jnp.bfloat16)
 
-    def rows(index):
+    def out_rows(index):
         return c_ref.at[pl.ds(pl.multiple_of(index * PART, PART), PART), :]
 
     place = out_ref.at[:, pl.ds(pl.multiple_of(t * CH, 128), CH)]
-    back = [remote(rows(tps[j][1]), place, a_send.at[j], a_recv.at[j], tps[j]) for j in range(NT - 1)]
+    back = [remote(out_rows(tps[j][1]), place, b_send.at[j], b_recv.at[j], tps[j]) for j in range(NT - 1)]
     for copy in back:
         copy.start()
-    mine = pltpu.make_async_copy(rows(t), place, loc.at[0])
+    mine = pltpu.make_async_copy(out_rows(t), place, loc.at[5])
     mine.start()
     mine.wait()
     for copy in back:
         copy.wait_recv()
-    for copy in copies + back:
+    for copy in pending + copies + back:
         copy.wait_send()
 
 
-def attend(qa, k2, v2, gk, gv, cosine, sine, bias, offset):
+def attend(q, k, v, pk, pv, cosine, sine, bias, offset):
     f32, bf = jnp.float32, jnp.bfloat16
     dma = pltpu.SemaphoreType.DMA
     return pl.pallas_call(
@@ -335,26 +353,41 @@
         out_shape=(
             jax.ShapeDtypeStruct((PART, NT * CH), bf),
             jax.ShapeDtypeStruct((TOK, CH), bf),
+            jax.ShapeDtypeStruct((TOK, CH), bf),
         ),
         in_specs=[pl.BlockSpec(memory_space=VMEM)] * 9,
-        out_specs=[pl.BlockSpec(memory_space=VMEM)] * 2,
+        out_specs=[pl.BlockSpec(memory_space=VMEM)] * 3,
         scratch_shapes=[
-            VMEM((CH, KEYS), bf),
+            VMEM((NX, TOK, CH), bf),
+            VMEM((2, TOK, CH), bf),
+            VMEM((2, TOK, CH), bf),
+            VMEM((NY, NZ, PAGE, CH), bf),
+            VMEM((NY, NZ, PAGE, CH), bf),
+            VMEM((NX, CH, TOK), bf),
+            VMEM((NY, CH, NZ * PAGE), bf),
             VMEM((CH, 2 * TOK), bf),
             VMEM((2 * TOK, CH), bf),
+            VMEM((NX, CH, TOK), f32),
+            VMEM((NX, 2 * HEADS, TOK), f32),
             VMEM((NX, CH, TOK), bf),
             VMEM((NX, 2 * HEADS, TOK), f32),
             VMEM((NX - 1, CH, TOK), bf),
             VMEM((NX - 1, 2 * HEADS, TOK), f32),
             VMEM((TOK, CH), bf),
+            dma((3, NT - 1)), dma((3, NT - 1)),
+            dma((2,)), dma((2,)),
+            dma((4, 4)), dma((4, 4)),
+            dma((4, 5)), dma((4, 5)),
+            dma((4,)), dma((4,)),
+            dma((2,)), dma((2,)),
             dma((NX - 1,)), dma((NX - 1,)),
             dma((NX - 1,)), dma((NX - 1,)),
             dma((NT - 1,)), dma((NT - 1,)),
-            dma((1,)),
+            dma((6,)),
         ],
-        compiler_params=pltpu.CompilerParams(collective_id=1, has_side_effects=True),
+        compiler_params=pltpu.CompilerParams(collective_id=0, has_side_effects=True),
         name="attend",
-    )(qa, k2, v2, gk, gv, cosine, sine, bias, offset)
+    )(q, k, v, pk, pv, cosine, sine, bias, offset)
 
 
 def tables(page_table, lengths, group_of):
@@ -380,18 +413,14 @@
     return (
         jnp.concatenate([cosine, cosine], axis=1),
         jnp.concatenate([-sine, sine], axis=1),
-        bias,
+        bias.reshape(NX, NY, NZ, TOK),
         offset[1][None, :],
     )
 
 
 def local(queries, keys, values, pool_keys, pool_values, page_table, lengths, group_of):
     cosine, sine, bias, offset = tables(page_table, lengths, group_of)
-    qa, k2, v2, gk, gv = spread(queries, keys, values, pool_keys, pool_values)
-    context, new_keys = attend(
-        qa, k2, v2, gk.reshape(KEYS, CH), gv.reshape(KEYS, CH), cosine, sine, bias, offset
-    )
-    return context, new_keys, v2[1]
+    return attend(queries, keys, values, pool_keys, pool_values, cosine, sine, bias, offset)
 
 
 def solution(mesh):

time: 114 us -> 101 us (0.89)
  Pallas kernels: 102 us -> 91.2 us
  other arithmetic: 4.95 us -> 3.65 us
    pallas_call x1 -> x0, Pallas kernels: 60 us -> none  [spread(): pl.pallas_call(spread_kernel, out_shape=(jax.ShapeDtypeStruct((NX, TOK, C...]
    pallas_call x1, Pallas kernels: 42.4 us -> 91.2 us  [attend(): pl.pallas_call(attend_kernel, out_shape=(jax.ShapeDtypeStruct((PART, NT *...]
    unnamed x4 -> x13, local copies, waits for them, and re-layouts: 3.24 us -> 4.65 us
where the time goes in v3:
time: 101 us
  Pallas kernels  91.2 us (90%)
  local copies, waits for them, and re-layouts  5.5 us (5%)
  other arithmetic  3.65 us (4%)
    pallas_call x1, Pallas kernels, attend(): pl.pallas_call(attend_kernel, out_shape=(jax.ShapeDtypeStruct((PART, NT *...  91.2 us
    unnamed x13, local copies, waits for them, and re-layouts  4.65 us

profile of v3, /device:TPU:1, one launch (start us, length us, event | category | flops | bytes accessed | tf_op | source)
XLA Modules:
  0.0 101.1 jit_solution(5088468563954161456)
XLA Ops:
  0.7 0.1 add_multiply_fusion
  0.7 0.0 copy-start.4
  0.8 0.7 copy-done.4
  1.4 0.1 slice.10
  1.5 0.2 compare_reduce_fusion
  1.7 0.1 reshape.125
  1.8 0.0 copy-start.2
  1.8 0.1 iota_add_fusion
  1.8 0.6 copy-done.2
  2.4 0.1 copy.13
  2.5 0.2 reduce-window.9
  2.7 0.1 reduce
  2.8 0.3 fusion.1
  3.1 0.1 add_convert_fusion
  3.2 0.0 copy-start.3
  3.2 0.6 slice.13.offset_ref
  3.7 0.1 copy-done.3
  3.8 0.2 select_reduce_fusion
  4.0 0.7 compare_select_fusion.1.bias_ref
  4.7 0.4 fusion.2
  5.2 0.7 pad_maximum_fusion.1.sin_ref
  5.9 0.7 pad_maximum_fusion.cos_ref
  6.5 91.2 %attend.1 = (bf16[32,3072]{1,0:T(8,128)(2,1)}, bf16[256,384]{1,0:T(8,128)(2,1)}, bf16[256,384]{1,0:T(8,128)(2,1)}) custom-call(bf16[32,3072]{1,0:T(8,128)(2,1)} %q_ref.1, bf16[32,3072]{1,0:T(8,128)(2,1)} %k_ref.1, bf16[32,3072]{1,0:T(8,128)(2,1)} %v_ref.1, bf16[1,128,384]{2,1,0:T(8,128)(2,1)} %pk_ref.1, bf16[1,128,384]{2,1,0:T(8,128)(2,1)} %pv_ref.1, ...), custom_call_target="tpu_custom_call" | custom-call | tf_op jit(solution)/shard_map/attend/pallas_call | solution.py:351
  97.7 0.0 copy-start.1
  97.7 1.7 %copy.17 = bf16[32,3072]{1,0:T(8,128)(2,1)} copy(bf16[32,3072]{1,0:T(8,128)(2,1)} %get-tuple-element.14) | data formatting | bytes 393216
  99.4 0.0 copy-done.1
  99.4 0.0 copy-start
  99.4 0.7 copy.18
  100.1 0.3 copy-done
  100.4 0.7 copy.19
  (6 shorter events, 0.0 us)
Async XLA Ops:
  0.7 0.7 copy-start.4
  1.8 0.7 copy-start.2
  3.2 0.7 copy-start.3
  97.7 1.7 %copy-start.1 = (bf16[256,384]{1,0:T(8,128)(2,1)S(1)}, bf16[256,384]{1,0:T(8,128)(2,1)}, u32[]{:S(2)}) copy-start(bf16[256,384]{1,0:T(8,128)(2,1)} %get-tuple-element.15) | copy-start | bytes 589828
  99.4 1.0 copy-start

commit v4 on v3

--- a/solution.py
+++ b/solution.py
@@ -1,5 +1,6 @@
 import jax
 import jax.numpy as jnp
+import numpy as np
 from jax import lax
 from jax.experimental import pallas as pl
 from jax.experimental.pallas import tpu as pltpu
@@ -66,9 +67,45 @@
     return jnp.concatenate(pieces, axis=0)
 
 
+def tables(page_ref, length_ref, group_ref, freq_ref, cos_ref, sin_ref, bias_ref, offset_ref):
+    s, t, x, y, z = where_am_i()
+    f32 = jnp.float32
+    count = length_ref.shape[1]
+    slots = page_ref.shape[1]
+    lane = lax.broadcasted_iota(jnp.int32, (count, count), 1)
+    line = lax.broadcasted_iota(jnp.int32, (count, count), 0)
+    lengths = jnp.broadcast_to(length_ref[...].astype(f32), (count, count))
+    groups = jnp.broadcast_to(group_ref[...].astype(f32), (count, count))
+    starts = jnp.sum(jnp.where(lane < line, lengths, 0.0), axis=1, keepdims=True)
+    ends = jnp.sum(jnp.where(lane <= line, lengths, 0.0), axis=1, keepdims=True)
+    group_of = jnp.sum(jnp.where(lane == line, groups, 0.0), axis=1, keepdims=True)
+    slot = lax.broadcasted_iota(jnp.int32, (COL, slots), 0) + x * COL
+    place = lax.broadcasted_iota(jnp.int32, (COL, slots), 1)
+    page = jnp.broadcast_to(page_ref[...], (COL, slots))
+    late = jnp.sum(jnp.where((page == slot) & (place >= slots // 2), 1.0, 0.0), axis=1, keepdims=True)
+    sign = jnp.where(lax.broadcasted_iota(jnp.int32, (ROT, TOK), 0) < HALF, -1.0, 1.0)
+    for i in range(2 + NX):
+        block = s - 1 + i if i < 2 else (i - 2) * COL + s % COL
+        rows = (block * TOK + lax.broadcasted_iota(jnp.int32, (1, TOK), 1)).astype(f32)
+        begun = starts <= rows
+        first = jnp.max(jnp.where(begun, starts, 0.0), axis=0, keepdims=True)
+        group = jnp.sum(jnp.where(begun & (rows < ends), group_of, 0.0), axis=0, keepdims=True)
+        offset = rows - first
+        angles = (COL * NX * PAGE // 2 + offset) * freq_ref[...]
+        cos_ref[i] = jnp.cos(angles)
+        sin_ref[i] = jnp.sin(angles) * sign
+        if i == 1:
+            offset_ref[...] = offset.astype(jnp.int32)
+        if i >= 2:
+            bias = jnp.where(group == late, 0.0, NEG)
+            for at in range(NY):
+                bias_ref[i - 2, at] = bias[at * NZ : (at + 1) * NZ]
+
+
 def attend_kernel(
-    q_ref, k_ref, v_ref, pk_ref, pv_ref, cos_ref, sin_ref, bias_ref, offset_ref,
+    q_ref, k_ref, v_ref, pk_ref, pv_ref, page_ref, length_ref, group_ref, freq_ref,
     out_ref, newk_ref, newv_ref,
+    cos_ref, sin_ref, bias_ref, offset_ref,
     qa_ref, k2_ref, v2_ref, gk_ref, gv_ref,
     qt_ref, vt_ref, vs_ref, ks_ref, acc_ref, run_ref, o_ref, stat_ref, ro_ref, rs_ref, c_ref,
     a_send, a_recv, z_send, z_recv, r_send, r_recv, y_send, y_recv, x_send, x_recv, s_send, s_recv,
@@ -149,17 +186,21 @@
                 )
 
     def hop(step):
-        hop_single(step)
-        if step == 0:
+        if step > 0:
+            hop_single(step)
+        else:
             zk.wait_recv()
             zv.wait_recv()
         for index, (ref, way, hops) in enumerate(flows):
             if last[index] is not None:
                 last[index].wait_recv()
                 last[index] = None
+            if step == 1:
+                early[index].wait_recv()
             if step < hops:
                 at = index_of(way, step)
-                block = ref.at[at] if ref is gk_ref else ref.at[at, :, low]
+                which = 1 - z if step == 0 else slice(None)
+                block = ref.at[at, which] if ref is gk_ref else ref.at[at, which, low]
                 last[index] = go(
                     remote(block, block, r_send.at[index, step], r_recv.at[index, step], up if way == 0 else down)
                 )
@@ -224,6 +265,14 @@
     def ahead(n):
         return (y + n) % NY
 
+    early = []
+    for index, (ref, way, hops) in enumerate(flows):
+        block = ref.at[y, z] if ref is gk_ref else ref.at[y, z, low]
+        early.append(
+            go(remote(block, block, r_send.at[index, 4], r_recv.at[index, 4], up if way == 0 else down))
+        )
+    hop_single(0)
+    tables(page_ref, length_ref, group_ref, freq_ref, cos_ref, sin_ref, bias_ref, offset_ref)
     hop(0)
     for copy in swaps[0]:
         copy.wait_recv()
@@ -239,9 +288,6 @@
         relays.append(go(remote(half, half, x_send.at[2 + i], x_recv.at[2 + i], to)))
     for copy in swaps[1] + swaps[2]:
         copy.wait_recv()
-    shifts = [
-        go(remote(ref.at[1], ref.at[0], s_send.at[i], s_recv.at[i], after)) for i, ref in enumerate((k2_ref, v2_ref))
-    ]
     newv_ref[...] = v2_ref[1]
     prepare((x + 1) % NX)
     prepare((x + 3) % NX)
@@ -256,6 +302,9 @@
     receive_values(2, [ahead(2), ahead(6)])
     absorb([ahead(2)])
     hop(3)
+    shifts = [
+        go(remote(ref.at[1], ref.at[0], s_send.at[i], s_recv.at[i], after)) for i, ref in enumerate((k2_ref, v2_ref))
+    ]
     absorb([ahead(6)])
     receive_values(3, [ahead(3), ahead(5)])
     absorb([ahead(3), ahead(5)])
@@ -345,8 +394,10 @@
         copy.wait_send()
 
 
-def attend(q, k, v, pk, pv, cosine, sine, bias, offset):
+def attend(q, k, v, pk, pv, pages, lengths, groups):
     f32, bf = jnp.float32, jnp.bfloat16
+    inverse_freq = (10000.0 ** (-(np.arange(HALF) * 2.0 / ROT))).astype(np.float32)
+    freq = jnp.asarray(np.concatenate([inverse_freq, inverse_freq])[:, None])
     dma = pltpu.SemaphoreType.DMA
     return pl.pallas_call(
         attend_kernel,
@@ -358,6 +409,10 @@
         in_specs=[pl.BlockSpec(memory_space=VMEM)] * 9,
         out_specs=[pl.BlockSpec(memory_space=VMEM)] * 3,
         scratch_shapes=[
+            VMEM((2 + NX, ROT, TOK), f32),
+            VMEM((2 + NX, ROT, TOK), f32),
+            VMEM((NX, NY, NZ, TOK), f32),
+            VMEM((1, TOK), jnp.int32),
             VMEM((NX, TOK, CH), bf),
             VMEM((2, TOK, CH), bf),
             VMEM((2, TOK, CH), bf),
@@ -376,7 +431,7 @@
             VMEM((TOK, CH), bf),
             dma((3, NT - 1)), dma((3, NT - 1)),
             dma((2,)), dma((2,)),
-            dma((4, 4)), dma((4, 4)),
+            dma((4, 5)), dma((4, 5)),
             dma((4, 5)), dma((4, 5)),
             dma((4,)), dma((4,)),
             dma((2,)), dma((2,)),
@@ -387,40 +442,13 @@
         ],
         compiler_params=pltpu.CompilerParams(collective_id=0, has_side_effects=True),
         name="attend",
-    )(q, k, v, pk, pv, cosine, sine, bias, offset)
-
-
-def tables(page_table, lengths, group_of):
-    s = lax.axis_index("seq")
-    x, col = s // COL, s % COL
-    blocks = jnp.concatenate([jnp.stack([s - 1, s]), jnp.arange(NX, dtype=jnp.int32) * COL + col])
-    rows = (blocks[:, None] * TOK + jnp.arange(TOK, dtype=jnp.int32)[None, :]).astype(jnp.int32)
-    starts = (jnp.cumsum(lengths) - lengths).astype(jnp.int32)
-    begun = starts[:, None, None] <= rows[None]
-    first = jnp.max(jnp.where(begun, starts[:, None, None], 0), axis=0)
-    ids = jnp.arange(lengths.shape[0], dtype=jnp.int32)
-    request = jnp.sum(begun.astype(jnp.int32), axis=0) - 1
-    group = jnp.sum(jnp.where(request[None] == ids[:, None, None], group_of[:, None, None], 0), axis=0)
-    offset = rows - first
-    position = (COL * NX * PAGE // 2 + offset).astype(jnp.float32)
-    inverse_freq = 10000.0 ** (-(jnp.arange(HALF, dtype=jnp.float32) * 2.0 / ROT))
-    angles = position[:, None, :] * inverse_freq[None, :, None]
-    cosine, sine = jnp.cos(angles), jnp.sin(angles)
-    slots = x * COL + jnp.arange(COL, dtype=jnp.int32)
-    late = page_table[page_table.shape[0] // 2 :]
-    slot_group = jnp.any(slots[:, None] == late[None, :], axis=1).astype(jnp.int32)
-    bias = jnp.where(group[2:, None, :] == slot_group[None, :, None], 0.0, NEG).astype(jnp.float32)
-    return (
-        jnp.concatenate([cosine, cosine], axis=1),
-        jnp.concatenate([-sine, sine], axis=1),
-        bias.reshape(NX, NY, NZ, TOK),
-        offset[1][None, :],
+    )(q, k, v, pk, pv, pages, lengths, groups, freq)
+
+
+def local(queries, keys, values, pool_keys, pool_values, page_table, lengths, group_of):
+    return attend(
+        queries, keys, values, pool_keys, pool_values, page_table[None, :], lengths[None, :], group_of[None, :]
     )
-
-
-def local(queries, keys, values, pool_keys, pool_values, page_table, lengths, group_of):
-    cosine, sine, bias, offset = tables(page_table, lengths, group_of)
-    return attend(queries, keys, values, pool_keys, pool_values, cosine, sine, bias, offset)
 
 
 def solution(mesh):

time: 101 us -> 99.5 us (0.985)
  Pallas kernels: 91.2 us -> 95.3 us
  other arithmetic: 3.65 us -> 0 us
  local copies, waits for them, and re-layouts: 5.5 us -> 3.33 us
    pallas_call x1, Pallas kernels: 91.2 us -> 95.3 us  [attend(): pl.pallas_call(attend_kernel, out_shape=(jax.ShapeDtypeStruct((PART, NT *...]
    concatenate x2 -> x0, other arithmetic: 1.36 us -> none  [the longest x1 0.68 us: tables(): jnp.concatenate([-sine, sine], axis=1)]
    unnamed x13 -> x7, local copies, waits for them, and re-layouts: 4.65 us -> 3.33 us
where the time goes in v4:
time: 99.5 us; the launch traced here: 99.3 us
  Pallas kernels  95.3 us (96%)
  local copies, waits for them, and re-layouts  3.33 us (3%)
    pallas_call x1, Pallas kernels, attend(): pl.pallas_call(attend_kernel, out_shape=(jax.ShapeDtypeStruct((PART, NT *...  95.3 us
    unnamed x7, local copies, waits for them, and re-layouts  3.33 us

profile of v4, /device:TPU:1, one launch (start us, length us, event | category | flops | bytes accessed | tf_op | source)
XLA Modules:
  0.0 99.3 jit_solution(17963444706303952720)
XLA Ops:
  0.6 95.3 %attend.1 = (bf16[32,3072]{1,0:T(8,128)(2,1)}, bf16[256,384]{1,0:T(8,128)(2,1)}, bf16[256,384]{1,0:T(8,128)(2,1)}) custom-call(bf16[32,3072]{1,0:T(8,128)(2,1)} %q_ref.1, bf16[32,3072]{1,0:T(8,128)(2,1)} %k_ref.1, bf16[32,3072]{1,0:T(8,128)(2,1)} %v_ref.1, bf16[1,128,384]{2,1,0:T(8,128)(2,1)} %pk_ref.1, bf16[1,128,384]{2,1,0:T(8,128)(2,1)} %pv_ref.1, ...), custom_call_target="tpu_custom_call" | custom-call | tf_op jit(solution)/shard_map/attend/pallas_call | solution.py:402
  96.0 0.0 copy-start.1
  96.0 1.7 %copy.15 = bf16[32,3072]{1,0:T(8,128)(2,1)} copy(bf16[32,3072]{1,0:T(8,128)(2,1)} %get-tuple-element.6) | data formatting | bytes 393216
  97.6 0.0 copy-done.1
  97.6 0.0 copy-start
  97.6 0.7 copy.16
  98.3 0.3 copy-done
  98.6 0.7 copy.17
Async XLA Ops:
  96.0 1.7 %copy-start.1 = (bf16[256,384]{1,0:T(8,128)(2,1)S(1)}, bf16[256,384]{1,0:T(8,128)(2,1)}, u32[]{:S(2)}) copy-start(bf16[256,384]{1,0:T(8,128)(2,1)} %get-tuple-element.7) | copy-start | bytes 589828
  97.6 1.0 %copy-start = (bf16[256,384]{1,0:T(8,128)(2,1)S(1)}, bf16[256,384]{1,0:T(8,128)(2,1)}, u32[]{:S(2)}) copy-start(bf16[256,384]{1,0:T(8,128)(2,1)} %get-tuple-element.8) | copy-start | bytes 589828

commit v5 on v4

--- a/solution.py
+++ b/solution.py
@@ -107,9 +107,9 @@
     out_ref, newk_ref, newv_ref,
     cos_ref, sin_ref, bias_ref, offset_ref,
     qa_ref, k2_ref, v2_ref, gk_ref, gv_ref,
-    qt_ref, vt_ref, vs_ref, ks_ref, acc_ref, run_ref, o_ref, stat_ref, ro_ref, rs_ref, c_ref,
+    qt_ref, vt_ref, vs_ref, ks_ref, acc_ref, run_ref, o_ref, stat_ref, ro_ref, rs_ref, rl_ref, c_ref,
     a_send, a_recv, z_send, z_recv, r_send, r_recv, y_send, y_recv, x_send, x_recv, s_send, s_recv,
-    o_send, o_recv, t_send, t_recv, b_send, b_recv, loc,
+    o_send, o_recv, f_send, f_recv, t_send, t_recv, b_send, b_recv, loc,
 ):
     s, t, x, y, z = where_am_i()
     col = s % COL
@@ -151,14 +151,15 @@
     ]
     for copy in own:
         copy.start()
-    swaps = []
-    for kind, (src, dst) in enumerate(kinds):
-        swaps.append(
-            [
-                go(remote(lanes(src, tps[j][1]), rows(dst, kind), a_send.at[kind, j], a_recv.at[kind, j], tps[j]))
-                for j in range(NT - 1)
-            ]
-        )
+
+    def swap(kind):
+        src, dst = kinds[kind]
+        return [
+            go(remote(lanes(src, tps[j][1]), rows(dst, kind), a_send.at[kind, j], a_recv.at[kind, j], tps[j]))
+            for j in range(NT - 1)
+        ]
+
+    query_swap = swap(0)
     for copy in own:
         copy.wait()
 
@@ -274,53 +275,61 @@
     hop_single(0)
     tables(page_ref, length_ref, group_ref, freq_ref, cos_ref, sin_ref, bias_ref, offset_ref)
     hop(0)
-    for copy in swaps[0]:
+    for copy in query_swap:
         copy.wait_recv()
     across = [
         go(remote(qa_ref.at[x], qa_ref.at[x], x_send.at[i], x_recv.at[i], to)) for i, to in enumerate((east, west))
     ]
-    prepare(x)
+    other_swaps = swap(1) + swap(2)
     hop(1)
     relays = []
     for i, to in enumerate((east, west)):
         across[i].wait_recv()
         half = qa_ref.at[(x + NX - 1) % NX if i == 0 else (x + 1) % NX, pl.ds(i * (TOK // 2), TOK // 2), :]
         relays.append(go(remote(half, half, x_send.at[2 + i], x_recv.at[2 + i], to)))
-    for copy in swaps[1] + swaps[2]:
-        copy.wait_recv()
-    newv_ref[...] = v2_ref[1]
+    prepare(x)
     prepare((x + 1) % NX)
     prepare((x + 3) % NX)
     receive_values(0, [y])
+    for copy in relays:
+        copy.wait_recv()
+    prepare((x + 2) % NX)
+    hop(2)
+    absorb([y], True)
     receive_values(1, [ahead(1), ahead(7)])
-    for copy in relays:
-        copy.wait_recv()
-    prepare((x + 2) % NX)
-    absorb([y], True)
-    hop(2)
     absorb([ahead(1), ahead(7)])
-    receive_values(2, [ahead(2), ahead(6)])
-    absorb([ahead(2)])
     hop(3)
+    for copy in other_swaps:
+        copy.wait_recv()
     shifts = [
         go(remote(ref.at[1], ref.at[0], s_send.at[i], s_recv.at[i], after)) for i, ref in enumerate((k2_ref, v2_ref))
     ]
-    absorb([ahead(6)])
+    newv_ref[...] = v2_ref[1]
+    receive_values(2, [ahead(2), ahead(6)])
+    absorb([ahead(2), ahead(6)])
+    hop(4)
     receive_values(3, [ahead(3), ahead(5)])
     absorb([ahead(3), ahead(5)])
-    hop(4)
     receive_values(4, [ahead(4)])
 
-    def hand_over(j):
-        b = (x + NX - 1 - j) % NX
-        to = (b * COL + col, t)
-        return [
-            remote(stat_ref.at[b], rs_ref.at[j], t_send.at[j], t_recv.at[j], to),
-            remote(o_ref.at[b], ro_ref.at[j], o_send.at[j], o_recv.at[j], to),
-        ]
+    def hand_stat(slot):
+        b = (x + NX - 1 - slot) % NX
+        return remote(stat_ref.at[b], rs_ref.at[slot], t_send.at[slot], t_recv.at[slot], (b * COL + col, t))
+
+    def hand_near(slot):
+        b = (x + NX - 1 - slot) % NX
+        return remote(o_ref.at[b], ro_ref.at[slot], o_send.at[slot], o_recv.at[slot], (b * COL + col, t))
+
+    def hand_far(i):
+        half = o_ref.at[(x + 2) % NX, pl.ds(i * (CH // 2), CH // 2), :]
+        return remote(half, rl_ref.at[i], f_send.at[i], f_recv.at[i], (east, west)[i])
+
+    def pass_on(i):
+        place = ro_ref.at[1, pl.ds(i * (CH // 2), CH // 2), :]
+        return remote(rl_ref.at[i], place, f_send.at[2 + i], f_recv.at[2 + i], (east, west)[i])
 
     def close(j, carry):
-        b = (x + NX - 1 - j) % NX
+        b = (x + 2 + j) % NX
         for h in range(HEADS):
             top, total, summed = update(b, h, [ahead(4)], False)
             o_ref[b, h * HD : (h + 1) * HD, :] = (summed / total).astype(jnp.bfloat16)
@@ -328,9 +337,14 @@
             stat_ref[b, HEADS + h : HEADS + h + 1, :] = total
             if h == 0:
 
-                @pl.when(j > 0)
+                @pl.when(j == 1)
                 def _():
-                    for copy in hand_over(j - 1):
+                    for copy in (hand_far(0), hand_far(1), hand_stat(1)):
+                        copy.start()
+
+                @pl.when(j == 2)
+                def _():
+                    for copy in (hand_near(0), hand_stat(0)):
                         copy.start()
 
         return carry
@@ -343,7 +357,13 @@
         turned = turn(k2_ref[b].astype(jnp.float32).T, cos_ref[b], sin_ref[b])
         ks_ref[b * TOK : (b + 1) * TOK, :] = turned.T.astype(jnp.bfloat16)
         vs_ref[:, b * TOK : (b + 1) * TOK] = v2_ref[b].astype(jnp.float32).T.astype(jnp.bfloat16)
+        if b == 0:
+            for copy in (hand_near(2), hand_stat(2)):
+                copy.start()
     newk_ref[...] = ks_ref[TOK:, :]
+    for i in range(2):
+        hand_far(i).wait_recv()
+        pass_on(i).start()
     columns = qt_ref[x]
     token = lax.broadcasted_iota(jnp.int32, (2 * TOK, TOK), 1) + TOK
     key = lax.broadcasted_iota(jnp.int32, (2 * TOK, TOK), 0)
@@ -357,7 +377,8 @@
         total, summed = weigh(scores, top, [vs_ref[h * HD : (h + 1) * HD, :]])
         suffix.append((top, total, summed / total))
 
-    copies = [copy for j in range(NX - 1) for copy in hand_over(j)]
+    far = [hand_far(0), hand_far(1)]
+    copies = [hand_near(0), hand_near(2), pass_on(0), pass_on(1)] + [hand_stat(slot) for slot in range(NX - 1)]
     for copy in copies:
         copy.wait_recv()
     heads = []
@@ -390,7 +411,7 @@
     mine.wait()
     for copy in back:
         copy.wait_recv()
-    for copy in pending + copies + back:
+    for copy in pending + far + copies + back:
         copy.wait_send()
 
 
@@ -428,6 +449,7 @@
             VMEM((NX, 2 * HEADS, TOK), f32),
             VMEM((NX - 1, CH, TOK), bf),
             VMEM((NX - 1, 2 * HEADS, TOK), f32),
+            VMEM((2, CH // 2, TOK), bf),
             VMEM((TOK, CH), bf),
             dma((3, NT - 1)), dma((3, NT - 1)),
             dma((2,)), dma((2,)),
@@ -436,6 +458,7 @@
             dma((4,)), dma((4,)),
             dma((2,)), dma((2,)),
             dma((NX - 1,)), dma((NX - 1,)),
+            dma((4,)), dma((4,)),
             dma((NX - 1,)), dma((NX - 1,)),
             dma((NT - 1,)), dma((NT - 1,)),
             dma((6,)),

time: 99.5 us -> 91 us (0.915)
  Pallas kernels: 95.3 us -> 85.9 us
    pallas_call x1, Pallas kernels: 95.3 us -> 85.9 us  [attend(): pl.pallas_call(attend_kernel, out_shape=(jax.ShapeDtypeStruct((PART, NT *...]
where the time goes in v5:
time: 91 us; the launch traced here: 89.9 us
  Pallas kernels  85.9 us (94%)
  local copies, waits for them, and re-layouts  3.33 us (4%)
    pallas_call x1, Pallas kernels, attend(): pl.pallas_call(attend_kernel, out_shape=(jax.ShapeDtypeStruct((PART, NT *...  85.9 us
    unnamed x7, local copies, waits for them, and re-layouts  3.33 us

profile of v5, /device:TPU:1, one launch (start us, length us, event | category | flops | bytes accessed | tf_op | source)
XLA Modules:
  0.0 89.9 jit_solution(10310373309958484885)
XLA Ops:
  0.6 85.9 %attend.1 = (bf16[32,3072]{1,0:T(8,128)(2,1)}, bf16[256,384]{1,0:T(8,128)(2,1)}, bf16[256,384]{1,0:T(8,128)(2,1)}) custom-call(bf16[32,3072]{1,0:T(8,128)(2,1)} %q_ref.1, bf16[32,3072]{1,0:T(8,128)(2,1)} %k_ref.1, bf16[32,3072]{1,0:T(8,128)(2,1)} %v_ref.1, bf16[1,128,384]{2,1,0:T(8,128)(2,1)} %pk_ref.1, bf16[1,128,384]{2,1,0:T(8,128)(2,1)} %pv_ref.1, ...), custom_call_target="tpu_custom_call" | custom-call | tf_op jit(solution)/shard_map/attend/pallas_call | solution.py:423
  86.6 0.0 copy-start.1
  86.6 1.7 %copy.15 = bf16[32,3072]{1,0:T(8,128)(2,1)} copy(bf16[32,3072]{1,0:T(8,128)(2,1)} %get-tuple-element.6) | data formatting | bytes 393216
  88.3 0.0 copy-done.1
  88.3 0.0 copy-start
  88.3 0.7 copy.16
  88.9 0.3 copy-done
  89.3 0.7 copy.17
Async XLA Ops:
  86.6 1.7 %copy-start.1 = (bf16[256,384]{1,0:T(8,128)(2,1)S(1)}, bf16[256,384]{1,0:T(8,128)(2,1)}, u32[]{:S(2)}) copy-start(bf16[256,384]{1,0:T(8,128)(2,1)} %get-tuple-element.7) | copy-start | bytes 589828
  88.3 1.0 %copy-start = (bf16[256,384]{1,0:T(8,128)(2,1)S(1)}, bf16[256,384]{1,0:T(8,128)(2,1)}, u32[]{:S(2)}) copy-start(bf16[256,384]{1,0:T(8,128)(2,1)} %get-tuple-element.8) | copy-start | bytes 589828

commit v6 on v5

--- a/solution.py
+++ b/solution.py
@@ -252,8 +252,9 @@
             summed += acc_ref[b, part, :] * factor
         return top, total, summed
 
-    def absorb(places, first=False):
-        def one(b, carry):
+    def absorb(places, first=False, start=0, stop=NX):
+        def one(n, carry):
+            b = (x + n) % NX
             for h in range(HEADS):
                 top, total, summed = update(b, h, places, first)
                 run_ref[b, h : h + 1, :] = top
@@ -261,7 +262,7 @@
                 acc_ref[b, h * HD : (h + 1) * HD, :] = summed
             return carry
 
-        lax.fori_loop(0, NX, one, 0)
+        lax.fori_loop(start, stop, one, 0)
 
     def ahead(n):
         return (y + n) % NY
@@ -282,20 +283,23 @@
     ]
     other_swaps = swap(1) + swap(2)
     hop(1)
+    prepare(x)
+    receive_values(0, [y])
     relays = []
     for i, to in enumerate((east, west)):
         across[i].wait_recv()
         half = qa_ref.at[(x + NX - 1) % NX if i == 0 else (x + 1) % NX, pl.ds(i * (TOK // 2), TOK // 2), :]
         relays.append(go(remote(half, half, x_send.at[2 + i], x_recv.at[2 + i], to)))
-    prepare(x)
+    absorb([y], True, 0, 1)
     prepare((x + 1) % NX)
+    absorb([y], True, 1, 2)
     prepare((x + 3) % NX)
-    receive_values(0, [y])
+    absorb([y], True, 3, 4)
     for copy in relays:
         copy.wait_recv()
+    hop(2)
     prepare((x + 2) % NX)
-    hop(2)
-    absorb([y], True)
+    absorb([y], True, 2, 3)
     receive_values(1, [ahead(1), ahead(7)])
     absorb([ahead(1), ahead(7)])
     hop(3)

time: 91 us -> 89.9 us (0.988)
  no operation moved by 1% of the time
where the time goes in v6:
time: 89.9 us; the launch traced here: 89.7 us
  Pallas kernels  85.7 us (95%)
  local copies, waits for them, and re-layouts  3.33 us (4%)
    pallas_call x1, Pallas kernels, attend(): pl.pallas_call(attend_kernel, out_shape=(jax.ShapeDtypeStruct((PART, NT *...  85.7 us
    unnamed x7, local copies, waits for them, and re-layouts  3.33 us

profile of v6, /device:TPU:1, one launch (start us, length us, event | category | flops | bytes accessed | tf_op | source)
XLA Modules:
  0.0 89.7 jit_solution(15005367730277467858)
XLA Ops:
  0.6 85.7 %attend.1 = (bf16[32,3072]{1,0:T(8,128)(2,1)}, bf16[256,384]{1,0:T(8,128)(2,1)}, bf16[256,384]{1,0:T(8,128)(2,1)}) custom-call(bf16[32,3072]{1,0:T(8,128)(2,1)} %q_ref.1, bf16[32,3072]{1,0:T(8,128)(2,1)} %k_ref.1, bf16[32,3072]{1,0:T(8,128)(2,1)} %v_ref.1, bf16[1,128,384]{2,1,0:T(8,128)(2,1)} %pk_ref.1, bf16[1,128,384]{2,1,0:T(8,128)(2,1)} %pv_ref.1, ...), custom_call_target="tpu_custom_call" | custom-call | tf_op jit(solution)/shard_map/attend/pallas_call | solution.py:427
  86.4 0.0 copy-start.1
  86.4 1.7 %copy.15 = bf16[32,3072]{1,0:T(8,128)(2,1)} copy(bf16[32,3072]{1,0:T(8,128)(2,1)} %get-tuple-element.6) | data formatting | bytes 393216
  88.0 0.0 copy-done.1
  88.0 0.0 copy-start
  88.0 0.7 copy.16
  88.7 0.3 copy-done
  89.0 0.7 copy.17
Async XLA Ops:
  86.4 1.7 %copy-start.1 = (bf16[256,384]{1,0:T(8,128)(2,1)S(1)}, bf16[256,384]{1,0:T(8,128)(2,1)}, u32[]{:S(2)}) copy-start(bf16[256,384]{1,0:T(8,128)(2,1)} %get-tuple-element.7) | copy-start | bytes 589828
  88.0 1.0 %copy-start = (bf16[256,384]{1,0:T(8,128)(2,1)S(1)}, bf16[256,384]{1,0:T(8,128)(2,1)}, u32[]{:S(2)}) copy-start(bf16[256,384]{1,0:T(8,128)(2,1)} %get-tuple-element.8) | copy-start | bytes 589828
